TPU v7x, 256 devices: a whole 4x4x8 slice. The times are simulated.
256 devices in a mesh: ent: 64 (over x, y, z_hi), rel: 4 (over z_lo, core).
Axes of the slice: x: 4, y: 4, z: 8 (z_hi: 4, z_lo: 2; z = z_hi * 2 + z_lo), core: 2. Of those that a mesh axis runs over, the one named last changes fastest.
Arguments:
- entity_table: bfloat16 [1024, 1024], P('ent'), may hold values from -1.5 to 1.5
- phases: float32 [4096, 512], P('rel'), may hold values from -3.140625 to 3.140625
- head_owner: int32 [131072, 1], P(('ent', 'rel')), may hold values from 0 to 255; in each aligned block of 512 rows (0 to 511, 512 to 1023, ...) at most 4 rows name the same one
- head_row: int32 [131072], P(('ent', 'rel')), may hold values from 0 to 3
- relation: int32 [131072], P(('ent', 'rel')), may hold values from 0 to 1023
- tail_ids: int32 [131072], P(('ent', 'rel')), may hold values from 0 to 1023
- known_tails: int32 [131072, 32], P(('ent', 'rel')), may hold values from 0 to 1023
Outputs:
- entity_gradient: float32 [1024, 1024], P(('ent', 'rel'))
- relation_gradient: float32 [4096, 512], P('rel')
Inputs may be any that keep to these rules, and one draw needn't show every extreme that they name: `head_owner`: owner o of the 256 holds working-set rows o * 4 to o * 4 + 3 and is device (o // 4, o mod 4) of ent and rel. Among the 512 triples of one device at most 4 have heads held by one owner, and exactly 4 in some devices. The triples of block b of 512 belong to relation group b mod 4.
All inputs are finite; a program needn't handle non-finite values.
Results may differ from a plain program's by a relative error of at most 0.004.
Values may be sent and summed in bfloat16 or wider, within the bound.
A program may use at most 64 MiB of HBM per device.

v0:
```python
import jax
import jax.numpy as jnp
from jax import lax
from jax.sharding import PartitionSpec as P


def local(entity_table, phases, head_owner, head_row, relation, tail_ids, known_tails):
    n_ent = lax.axis_size("ent")
    n_rel = lax.axis_size("rel")
    owner_count = n_ent * n_rel
    rows_dev = head_row.shape[0]
    owner_rows = entity_table.shape[0] // n_rel
    half = phases.shape[1]
    width = 2 * half
    table_all = lax.all_gather(entity_table, "ent", axis=0, tiled=True)
    entities = table_all.shape[0]
    table_sq = jnp.sum(jnp.square(table_all.astype(jnp.float32)), axis=1)
    columns = lax.broadcasted_iota(jnp.int32, (1, entities), 1)
    heads = head_owner[:, 0] * owner_rows + head_row
    head_f = table_all[heads].astype(jnp.float32)
    angles = phases[relation]
    cosine = jnp.cos(angles)
    sine_part = jnp.sin(angles)
    head_re = head_f[:, :half]
    head_im = head_f[:, half:]
    query_re = head_re * cosine - head_im * sine_part
    query_im = head_re * sine_part + head_im * cosine
    query = jnp.concatenate([query_re, query_im], axis=1).astype(jnp.bfloat16)
    query_f = query.astype(jnp.float32)
    query_sq = jnp.sum(query_f * query_f, axis=1)
    cross = lax.dot_general(
        query, table_all, (((1,), (1,)), ((), ())), preferred_element_type=jnp.float32
    )
    scores = 2.0 * cross - query_sq[:, None] - table_sq[None, :]
    listed = jnp.zeros(scores.shape, jnp.bool_)
    for column_j in range(known_tails.shape[1]):
        listed = listed | (known_tails[:, column_j : column_j + 1] == columns)
    is_target = columns == tail_ids[:, None]
    masked = listed & jnp.logical_not(is_target)
    row_max = jnp.max(jnp.where(masked, -jnp.inf, scores), axis=1)
    raw_prob = jnp.where(masked, 0.0, jnp.exp(scores - row_max[:, None]))
    prob = raw_prob / jnp.sum(raw_prob, axis=1, keepdims=True)
    weights = (prob - is_target.astype(jnp.float32)).astype(jnp.bfloat16)
    dquery = 2.0 * jnp.dot(weights, table_all, preferred_element_type=jnp.float32)
    grad_re = dquery[:, :half]
    grad_im = dquery[:, half:]
    head_rows = jnp.concatenate(
        [grad_re * cosine + grad_im * sine_part, -grad_re * sine_part + grad_im * cosine], axis=1
    ).astype(jnp.bfloat16)
    dangle = -query_im * grad_re + query_re * grad_im
    rel_local = jax.ops.segment_sum(dangle, relation, num_segments=phases.shape[0])
    relation_gradient = lax.psum(rel_local, "ent")
    counts = jnp.sum(weights.astype(jnp.float32), axis=0)
    cross_t = lax.dot_general(
        weights, query, (((0,), (0,)), ((), ())), preferred_element_type=jnp.float32
    )
    result = 2.0 * (cross_t - counts[:, None] * table_all.astype(jnp.float32))
    summed = lax.psum_scatter(result, ("ent", "rel"), scatter_dimension=0, tiled=True)
    capacity = 2 * rows_dev // owner_count
    owners = head_owner[:, 0]
    owner_hot = (owners[:, None] == lax.broadcasted_iota(jnp.int32, (1, owner_count), 1)).astype(
        jnp.int32
    )
    earlier = jnp.cumsum(owner_hot, axis=0) - owner_hot
    position = jnp.sum(earlier * owner_hot, axis=1)
    slot_ids = owners * capacity + position
    send_rows = jnp.zeros((owner_count * capacity, width), jnp.bfloat16).at[slot_ids].set(head_rows)
    send_labels = jnp.full((owner_count * capacity,), -1, jnp.int32).at[slot_ids].set(head_row)
    recv_rows, recv_labels = (
        lax.all_to_all(
            lax.all_to_all(
                send_rows.reshape(n_ent, n_rel, capacity, width),
                "ent",
                split_axis=0,
                concat_axis=0,
                tiled=True,
            ),
            "rel",
            split_axis=1,
            concat_axis=1,
            tiled=True,
        ),
        lax.all_to_all(
            lax.all_to_all(
                send_labels.reshape(n_ent, n_rel, capacity),
                "ent",
                split_axis=0,
                concat_axis=0,
                tiled=True,
            ),
            "rel",
            split_axis=1,
            concat_axis=1,
            tiled=True,
        ),
    )
    picks = (
        recv_labels.reshape(1, -1) == lax.broadcasted_iota(jnp.int32, (owner_rows, 1), 0)
    ).astype(jnp.bfloat16)
    summed = summed + jnp.dot(
        picks, recv_rows.reshape(-1, width), preferred_element_type=jnp.float32
    )
    return (summed, relation_gradient)


def solution(mesh):
    in_specs = (
        P("ent", None),
        P("rel", None),
        P(("ent", "rel"), None),
        P(("ent", "rel")),
        P(("ent", "rel")),
        P(("ent", "rel")),
        P(("ent", "rel"), None),
    )
    out_specs = (P(("ent", "rel"), None), P("rel", None))
    return jax.shard_map(local, mesh=mesh, in_specs=in_specs, out_specs=out_specs, check_vma=False)
```

profile of v0, /device:TPU:32, one launch (start us, length us, event | category | flops | bytes accessed | tf_op | source)
XLA Modules:
  0.0 1178.3 jit_solution(7030112479084193069)
XLA Ops:
  9.4 2.4 scatter_custom_fusion
  12.7 13.7 %all-to-all-start = ((s32[64,4,4]{2,1,0:T(4,128)}), s32[64,4,4]{2,1,0:T(4,128)S(1)}, u32[]{:S(2)}, u32[]{:S(2)}) async-start(s32[64,4,4]{2,1,0:T(4,128)} %reshape.39), calls=%async_computation | async-start | bytes 262144 | tf_op jit(solution)/shard_map/all_to_all | solution.py:84
  26.5 2.3 gather_fusion.1
  28.9 5.5 fusion.64
  34.3 57.0 %all-gather.2.cloned.1.call-done = bf16[1024,1024]{1,0:T(8,128)(2,1)} async-done(((bf16[16,1024]{1,0:T(8,128)(2,1)}), bf16[1024,1024]{1,0:T(8,128)(2,1)}) %all-gather.2.cloned.1.call-update) | async-done | bytes 2097168 | tf_op jit(solution)/shard_map/all_gather | solution.py:15
  91.4 5.3 gather_fusion
  98.3 1.8 fusion.62
  100.9 13.2 %select_reduce_fusion = (f32[512]{0:T(512)S(1)}, pred[512,1024]{1,0:T(8,128)(4,1)S(1)}, f32[512,1024]{1,0:T(8,128)S(1)}) fusion(f32[1024]{0:T(1024)S(1)} %fusion, f32[512]{0:T(512)S(1)} %multiply_reduce_fusion, s32[512]{0:T(512)S(1)} %copy-done.12, s32[512]{0:T(512)S(1)} %bitcast.99, s32[512]{0:T(512)S(1)} %bitcast.100, s32[512]{0:T(512)S(1)} %bitcast.70, ...), kind=kOutput, calls=%fused_computation.13 | convolution fusion | flops 1113062912 | bytes 5842944 | tf_op jit(solution)/shard_map/dot_general | solution.py:31
  119.3 4.8 scatter_custom_fusion.1
  124.0 4.1 reshape.40
  128.2 10.4 all-to-all-start.2
  138.7 5.2 fusion.2
  144.7 51.1 %all-to-all-done.2 = bf16[64,4,4,1024]{3,2,1,0:T(4,128)(2,1)} async-done(((bf16[64,4,4,1024]{3,2,1,0:T(4,128)(2,1)}), bf16[64,4,4,1024]{3,2,1,0:T(4,128)(2,1)}, u32[]{:S(2)}, u32[]{:S(2)}) %all-to-all-start.2) | async-done | bytes 2097184 | tf_op jit(solution)/shard_map/all_to_all | solution.py:71
  195.9 4.7 all-to-all-start.1
  200.6 3.7 copy.20
  204.3 4.9 all-to-all-start.3
  209.2 6.5 scatter_custom_fusion.2
  217.3 17.5 %all-to-all-done.3 = bf16[64,4,4,1024]{3,2,0,1:T(4,128)(2,1)} async-done(((bf16[64,4,4,1024]{3,2,0,1:T(4,128)(2,1)}), bf16[64,4,4,1024]{3,2,0,1:T(4,128)(2,1)}, u32[]{:S(2)}, u32[]{:S(2)}) %all-to-all-start.3) | async-done | bytes 2097184 | tf_op jit(solution)/shard_map/all_to_all | solution.py:70
  234.7 4.2 copy.21
  238.9 4.0 reshape.41
  242.9 182.1 %all-reduce.6.cloned.1.call-done = f32[1024,1024]{1,0:T(8,128)} async-done(((f32[1024,1024]{1,0:T(8,128)}), f32[1024,1024]{1,0:T(8,128)}) %all-reduce.6.cloned.1.call-update) | async-done | bytes 4194320
  425.0 2.6 convolution_add_fusion
  427.5 741.1 %all-reduce.4.cloned.1.call-done = f32[1024,512]{1,0:T(8,128)} async-done(((f32[1024,512]{1,0:T(8,128)}), f32[1024,512]{1,0:T(8,128)}) %all-reduce.4.cloned.1.call-update) | async-done | bytes 2097168 | tf_op jit(solution)/shard_map/psum | solution.py:52
  1168.7 3.1 copy.24
  (69 shorter events, 12.9 us)
Async XLA Ops:
  7.2 19.3 %copy-start = (f32[1024,512]{1,0:T(8,128)S(1)}, f32[1024,512]{1,0:T(8,128)}, u32[]{:S(2)}) copy-start(f32[1024,512]{1,0:T(8,128)} %param.8) | copy-start | bytes 6291460
  7.2 2.0 copy-start.11
  7.2 2.2 copy-start.13
  7.2 19.2 %copy-start.14 = (s32[512]{0:T(512)S(1)}, s32[512]{0:T(512)}, u32[]{:S(2)}) copy-start(s32[512]{0:T(512)} %param.11) | copy-start | bytes 6148
  7.2 84.1 %all-gather.2.cloned.1.call-start = ((), (), s32[]{:S(2)}) async-start(), calls=%async_computation.4 | async-start | bytes 2129920 | tf_op jit(solution)/shard_map/all_gather | solution.py:15
  12.7 115.5 %all-to-all-start = ((s32[64,4,4]{2,1,0:T(4,128)}), s32[64,4,4]{2,1,0:T(4,128)S(1)}, u32[]{:S(2)}, u32[]{:S(2)}) async-start(s32[64,4,4]{2,1,0:T(4,128)} %reshape.39), calls=%async_computation | async-start | bytes 262144 | tf_op jit(solution)/shard_map/all_to_all | solution.py:84
  26.4 2.4 copy-start.10
  96.7 1.6 copy-start.2
  98.3 2.1 copy-start.1
  100.1 14.0 %copy-start.5 = (bf16[512,512]{1,0:T(8,128)(2,1)}, bf16[512,512]{1,0:T(8,128)(2,1)S(1)}, u32[]{:S(2)}) copy-start(bf16[512,512]{1,0:T(8,128)(2,1)S(1)} %get-tuple-element.6) | copy-start | bytes 1572868
  100.1 14.0 %copy-start.7 = (bf16[512,512]{1,0:T(8,128)(2,1)}, bf16[512,512]{1,0:T(8,128)(2,1)S(1)}, u32[]{:S(2)}) copy-start(bf16[512,512]{1,0:T(8,128)(2,1)S(1)} %get-tuple-element.12) | copy-start | bytes 1572868
  100.1 0.8 copy-start.12
  116.3 1.3 copy-start.9
  117.6 1.7 copy-start.3
  128.2 10.5 copy-start.6
  128.2 10.5 copy-start.8
  128.2 67.7 %all-to-all-start.2 = ((bf16[64,4,4,1024]{3,2,1,0:T(4,128)(2,1)}), bf16[64,4,4,1024]{3,2,1,0:T(4,128)(2,1)}, u32[]{:S(2)}, u32[]{:S(2)}) async-start(bf16[64,4,4,1024]{3,2,1,0:T(4,128)(2,1)} %reshape.40), calls=%async_computation.2 | async-start | bytes 4194304 | tf_op jit(solution)/shard_map/all_to_all | solution.py:71
  138.6 286.3 %all-reduce.6.cloned.1.call-start = ((), (), s32[]{:S(2)}) async-start(), calls=%async_computation.6 | async-start | bytes 8388608
  195.9 8.5 all-to-all-start.1
  204.3 4.9 copy-start.4
  204.3 30.4 %all-to-all-start.3 = ((bf16[64,4,4,1024]{3,2,0,1:T(4,128)(2,1)}), bf16[64,4,4,1024]{3,2,0,1:T(4,128)(2,1)}, u32[]{:S(2)}, u32[]{:S(2)}) async-start(bf16[64,4,4,1024]{3,2,0,1:T(4,128)(2,1)} %copy.20), calls=%async_computation.3 | async-start | bytes 4194304 | tf_op jit(solution)/shard_map/all_to_all | solution.py:70
  209.2 959.5 %all-reduce.4.cloned.1.call-start = ((), (), s32[]{:S(2)}) async-start(), calls=%async_computation.5 | async-start | bytes 4194304 | tf_op jit(solution)/shard_map/psum | solution.py:52
Sparse Core Ops, SparseCore 0:
  11.3 79.9 all-gather.1
  144.9 280.0 all-reduce.5
  427.6 741.0 all-reduce.3
where the time goes:
time: 1180 us
  waiting for transfers between devices  1050 us (89%)
  local copies, waits for them, and re-layouts  38.3 us (3%)
  starting transfers between devices  33.8 us (3%)
  matrix products  22.3 us (2%)
  other arithmetic  20.4 us (2%)
  between operations  14 us (1%)
    psum x1, waiting for transfers between devices, local(): relation_gradient = lax.psum(rel_local, 'ent')  741 us
    unnamed x4, waiting for transfers between devices  183 us
    all_gather x1, waiting for transfers between devices, local(): table_all = lax.all_gather(entity_table, 'ent', axis=0, tiled=True)  57 us
    all_to_all x1, waiting for transfers between devices, local(): lax.all_to_all(send_rows.reshape(n_ent, n_rel, capacity, width), 'ent', s...  51.1 us
  transfers between devices with their start and end apart: 7, of which 5 were waited for; matrix products, arithmetic and copies ran while one was open for 7% of the time, Pallas kernels for 0%

commit v1 on v0

v1 whole, which is shorter than its diff:
```python
import functools

import jax
import jax.numpy as jnp
from jax import lax
from jax.experimental import pallas as pl
from jax.experimental.pallas import tpu as pltpu
from jax.sharding import PartitionSpec as P

MESH = pl.DeviceIdType.MESH
VMEM = pltpu.VMEM
F32 = jnp.float32
BF16 = jnp.bfloat16
WIRE = jnp.bfloat16
COLS = 512

SIN = (0.9999999999932018, -0.16666666657817392, 0.008333333144447052, -0.00019841254471923497,
       2.7556704311932283e-06, -2.5038717712098566e-08, 1.5896746642760318e-10, -6.610935072102146e-13)
COS = (0.9999999999990714, -0.4999999999846839, 0.041666666625163704, -0.0013888888455803566,
       2.480156464708791e-05, -2.755665269895137e-07, 2.0865211281170485e-09, -1.1353643820753535e-11,
       4.131574377242709e-14)


def horner(coefficients, t):
    value = jnp.full_like(t, coefficients[-1])
    for c in coefficients[-2::-1]:
        value = value * t + c
    return value


def place():
    e = lax.axis_index("ent")
    r = lax.axis_index("rel")
    return e // 16, (e // 4) % 4, e % 4, r // 2, r % 2


def device(x, y, zh, zl, core):
    return {"ent": x * 16 + y * 4 + zh, "rel": zl * 2 + core}


class Wire:
    def __init__(self, send, recv):
        self.send, self.recv = send, recv
        self.count = 0
        self.open = []

    def number(self):
        self.count += 1
        return self.count - 1

    def start(self, t, src, dst, to):
        copy = pltpu.make_async_remote_copy(
            src_ref=src, dst_ref=dst, send_sem=self.send.at[t], recv_sem=self.recv.at[t],
            device_id=to, device_id_type=MESH)
        copy.start()
        self.open.append(copy)

    def wait(self, t, dst, to):
        pltpu.make_async_remote_copy(
            src_ref=dst, dst_ref=dst, send_sem=self.send.at[t], recv_sem=self.recv.at[t],
            device_id=to, device_id_type=MESH).wait_recv()

    def drain(self):
        for copy in self.open:
            copy.wait_send()
        self.open = []


def greet(x, y, zh, zl, core):
    barrier = pltpu.get_barrier_semaphore()
    z = zh * 2 + zl
    peers = [device(x, y, zh, zl, 1 - core)]
    for d in (1, 3):
        peers.append(device((x + d) % 4, y, zh, zl, core))
        peers.append(device(x, (y + d) % 4, zh, zl, core))
    for d in range(1, 8):
        zz = (z + d) % 8
        peers.append(device(x, y, zz // 2, zz % 2, core))
    for peer in peers:
        pl.semaphore_signal(barrier, inc=1, device_id=peer, device_id_type=MESH)
    pl.semaphore_wait(barrier, len(peers))


class Spread:
    def __init__(self, wire, block, to, a0, b0, have):
        self.w, self.block, self.to, self.a0, self.b0, self.have = wire, block, to, a0, b0, have
        number = wire.number
        self.tb = [number() for _ in range(4)]
        self.ta = [[number() for _ in range(4)] for _ in range(4)]

    def half(self, a, b, h):
        return self.block(a, b).at[pl.ds(32 * h, 32)]

    def got(self, j):
        a0, b = self.a0, (self.b0 + j) % 4
        blk = self.block(a0, b)
        self.w.start(self.ta[j][0], blk, blk, self.to((a0 + 1) % 4, self.b0))
        self.w.start(self.ta[j][1], blk, blk, self.to((a0 + 3) % 4, self.b0))
        self.have(a0, b, j)

    def begin(self):
        a0, b0 = self.a0, self.b0
        blk = self.block(a0, b0)
        self.w.start(self.tb[0], blk, blk, self.to(a0, (b0 + 1) % 4))
        self.w.start(self.tb[1], blk, blk, self.to(a0, (b0 + 3) % 4))
        self.got(0)

    def along_b(self):
        a0, b0, w = self.a0, self.b0, self.w
        up, down = self.to(a0, (b0 + 1) % 4), self.to(a0, (b0 + 3) % 4)
        w.wait(self.tb[0], self.block(a0, (b0 + 3) % 4), down)
        part = self.half(a0, (b0 + 3) % 4, 0)
        w.start(self.tb[2], part, part, up)
        self.got(3)
        w.wait(self.tb[1], self.block(a0, (b0 + 1) % 4), up)
        part = self.half(a0, (b0 + 1) % 4, 1)
        w.start(self.tb[3], part, part, down)
        self.got(1)

    def along_b_far(self):
        a0, b0, w = self.a0, self.b0, self.w
        up, down = self.to(a0, (b0 + 1) % 4), self.to(a0, (b0 + 3) % 4)
        far = (b0 + 2) % 4
        w.wait(self.tb[2], self.half(a0, far, 0), down)
        w.wait(self.tb[3], self.half(a0, far, 1), up)
        self.got(2)

    def along_a(self, j):
        a0, w = self.a0, self.w
        b = (self.b0 + j) % 4
        up, down = self.to((a0 + 1) % 4, self.b0), self.to((a0 + 3) % 4, self.b0)
        t = self.ta[j]
        w.wait(t[0], self.block((a0 + 3) % 4, b), down)
        part = self.half((a0 + 3) % 4, b, 0)
        w.start(t[2], part, part, up)
        self.have((a0 + 3) % 4, b, 4 + j)
        w.wait(t[1], self.block((a0 + 1) % 4, b), up)
        part = self.half((a0 + 1) % 4, b, 1)
        w.start(t[3], part, part, down)
        self.have((a0 + 1) % 4, b, 8 + j)

    def along_a_far(self, j):
        a0, w = self.a0, self.w
        b = (self.b0 + j) % 4
        up, down = self.to((a0 + 1) % 4, self.b0), self.to((a0 + 3) % 4, self.b0)
        t = self.ta[j]
        far = (a0 + 2) % 4
        w.wait(t[2], self.half(far, b, 0), down)
        w.wait(t[3], self.half(far, b, 1), up)
        self.have(far, b, 12 + j)

    def rest(self):
        self.along_b()
        self.along_a(0)
        self.along_b_far()
        self.along_a(3)
        self.along_a(1)
        self.along_a_far(0)
        self.along_a(2)
        for j in (3, 1, 2):
            self.along_a_far(j)


class Collect:
    def __init__(self, wire, piece, to, m, bufs):
        self.w, self.piece, self.m, self.bufs = wire, piece, m, bufs
        self.up, self.down = to((m + 1) % 4), to((m + 3) % 4)
        self.t = [wire.number() for _ in range(6)]

    def begin(self):
        out, inn = self.bufs
        m, w = self.m, self.w
        far = (m + 2) % 4
        out[0] = self.piece(far, 0).astype(out.dtype)
        w.start(self.t[0], out.at[0], inn.at[0], self.up)
        out[1] = self.piece(far, 1).astype(out.dtype)
        w.start(self.t[1], out.at[1], inn.at[1], self.down)
        out[2] = self.piece((m + 1) % 4, 1).astype(out.dtype)
        w.start(self.t[2], out.at[2], inn.at[2], self.up)
        out[3] = self.piece((m + 3) % 4, 0).astype(out.dtype)
        w.start(self.t[3], out.at[3], inn.at[3], self.down)

    def middle(self):
        out, inn = self.bufs
        m, w = self.m, self.w
        w.wait(self.t[0], inn.at[0], self.down)
        out[4] = (self.piece((m + 1) % 4, 0) + inn[0].astype(F32)).astype(out.dtype)
        w.start(self.t[4], out.at[4], inn.at[4], self.up)
        w.wait(self.t[1], inn.at[1], self.up)
        out[5] = (self.piece((m + 3) % 4, 1) + inn[1].astype(F32)).astype(out.dtype)
        w.start(self.t[5], out.at[5], inn.at[5], self.down)

    def end(self):
        out, inn = self.bufs
        m, w = self.m, self.w
        w.wait(self.t[2], inn.at[2], self.down)
        w.wait(self.t[3], inn.at[3], self.up)
        w.wait(self.t[4], inn.at[4], self.down)
        w.wait(self.t[5], inn.at[5], self.up)
        first = self.piece(m, 0) + (inn[4].astype(F32) + inn[3].astype(F32))
        second = self.piece(m, 1) + (inn[2].astype(F32) + inn[5].astype(F32))
        return first, second


def gather_kernel(entity_ref, table_ref, send, recv, local_sem):
    x, y, zh, zl, core = place()
    z_sign = 2 * zl - 1
    mine = pl.ds(pl.multiple_of(core * COLS, COLS), COLS)
    greet(x, y, zh, zl, core)
    w = Wire(send, recv)
    a0 = x * (1 - core) + y * core
    b0 = y * (1 - core) + x * core

    def block(a, b):
        return table_ref.at[a * (1 - core) + b * core, b * (1 - core) + a * core, :, mine]

    def to(a, b):
        return device(a * (1 - core) + b * core, b * (1 - core) + a * core, zh, zl, core)

    partner = device(x, y, zh, zl, 1 - core)
    tp = [w.number() for _ in range(16)]
    tz = [w.number() for _ in range(3)]

    def have(a, b, j):
        w.start(tp[j], block(a, b), block(a, b), partner)

    def rows(k):
        return block(a0, b0).at[pl.ds(pl.multiple_of(k * 16, 16), 16)]

    own = pltpu.make_async_copy(entity_ref.at[:, mine], rows(zh), local_sem)
    own.start()
    z_to = [((zh + z_sign + 4) % 4, 1 - zl), ((zh + z_sign + 4) % 4, zl), ((zh + 2) % 4, 1 - zl)]
    for t, (h, l) in zip(tz, z_to):
        w.start(t, entity_ref.at[:, mine], rows(zh), device(x, y, h, l, core))
    z_from = [(zh + z_sign + 4) % 4, (zh - z_sign + 4) % 4, (zh + 2) % 4]
    for t, h in zip(tz, z_from):
        w.wait(t, rows(h), partner)
    own.wait()
    spread = Spread(w, block, to, a0, b0, have)
    spread.begin()
    spread.rest()
    other = 1 - core
    theirs = pl.ds(pl.multiple_of(other * COLS, COLS), COLS)
    for j in range(16):
        w.wait(tp[j], table_ref.at[0, 0, :, theirs], partner)
    w.drain()


def gather_table(entity_table):
    messages = 16 + 3 + 20
    table = pl.pallas_call(
        gather_kernel,
        out_shape=jax.ShapeDtypeStruct((4, 4, 64, 2 * COLS), BF16),
        in_specs=[pl.BlockSpec(memory_space=VMEM)],
        out_specs=pl.BlockSpec(memory_space=VMEM),
        scratch_shapes=[
            pltpu.SemaphoreType.DMA((messages,)),
            pltpu.SemaphoreType.DMA((messages,)),
            pltpu.SemaphoreType.DMA,
        ],
        compiler_params=pltpu.CompilerParams(collective_id=0, has_side_effects=True),
        name="gather_table",
    )(entity_table)
    return table.reshape(1024, 1024)


def reduce_kernel(g_ref, d_ref, e_ref, r_ref, send, recv, pair, g_acc, g_out, g_in, h_out, h_in, g_small, z_in,
                  g_last, g_swap, d_out, d_in, f_out, f_in, d_small, d_zin):
    x, y, zh, zl, core = place()
    z = zh * 2 + zl
    other = 1 - core
    greet(x, y, zh, zl, core)
    w = Wire(send, recv)
    partner = device(x, y, zh, zl, other)
    ga, gb = x * other + y * core, y * other + x * core
    da, db = gb, ga

    def gxy(a, b):
        return a * other + b * core, b * other + a * core

    def dxy(a, b):
        return b * other + a * core, a * other + b * core

    def gto(a, b):
        px, py = gxy(a, b)
        return device(px, py, zh, zl, core)

    def dto(a, b):
        px, py = dxy(a, b)
        return device(px, py, zh, zl, core)

    tp = {}
    order = [(i, j) for i in (2, 1, 3, 0) for j in range(4)]
    for i, j in order:
        tp[i, j] = w.number()

    def pair_xy(a, b):
        return dxy(a, b)

    for i, j in order:
        px, py = pair_xy((gb + i) % 4, j)
        w.start(tp[i, j], g_ref.at[other, px, py], pair.at[px, py], partner)

    def d_piece(c, h):
        parts = []
        for b in (2 * h, 2 * h + 1):
            px, py = dxy(c, b)
            parts.append(d_ref[px, py][None])
        return jnp.concatenate(parts, axis=0)

    d_first = Collect(w, d_piece, lambda a: dto(a, db), da, (d_out, d_in))
    d_first.begin()

    for i, j in order:
        px, py = gxy((ga + i) % 4, j)
        w.wait(tp[i, j], pair.at[px, py], partner)
        g_acc[i, j] = g_ref[core, px, py] + pair[px, py]

    def g_piece(c, h):
        i = (c - ga + 4) % 4
        return g_acc[i, pl.ds(2 * h, 2)]

    g_first = Collect(w, g_piece, lambda a: gto(a, gb), ga, (g_out, g_in))
    g_first.begin()
    d_first.middle()
    g_first.middle()

    first, second = d_first.end()
    d_small[0:2] = first
    d_small[2:4] = second

    def d_piece2(c, h):
        return d_small[c, 32 * h:32 * h + 32]

    d_second = Collect(w, d_piece2, lambda b: dto(da, b), db, (f_out, f_in))
    d_second.begin()

    first, second = g_first.end()
    g_small[0:2] = first
    g_small[2:4] = second

    def g_piece2(c, h):
        return g_small[c, 32 * h:32 * h + 32]

    g_second = Collect(w, g_piece2, lambda b: gto(ga, b), gb, (h_out, h_in))
    g_second.begin()
    d_second.middle()
    g_second.middle()

    first, second = d_second.end()
    d_small[0, 0:32] = first
    d_small[0, 32:64] = second
    tdz = [w.number() for _ in range(3)]
    for k in range(1, 4):
        hh = (zh + k) % 4
        src = d_small.at[0, pl.ds(pl.multiple_of(hh * 16, 16), 16)]
        w.start(tdz[k - 1], src, d_zin.at[k - 1], device(x, y, hh, zl, core))

    first, second = g_second.end()
    g_small[0, 0:32] = first
    g_small[0, 32:64] = second
    tgz = [w.number() for _ in range(7)]
    for k in range(1, 8):
        zz = (z + k) % 8
        src = g_small.at[0, pl.ds(pl.multiple_of(zz * 8, 8), 8)]
        w.start(tgz[k - 1], src, z_in.at[k - 1], device(x, y, zz // 2, zz % 2, core))

    def block(a, b):
        px, py = dxy(a, b)
        return r_ref.at[px, py]

    total = d_small[0, pl.ds(pl.multiple_of(zh * 16, 16), 16)]
    for k in range(1, 4):
        w.wait(tdz[k - 1], d_zin.at[k - 1], partner)
    total = total + ((d_zin[0] + d_zin[1]) + d_zin[2])

    def rows(k):
        return block(da, db).at[pl.ds(pl.multiple_of(k * 16, 16), 16)]

    rows(zh)[...] = total.astype(r_ref.dtype)
    trz = [w.number() for _ in range(3)]
    for k in range(1, 4):
        w.start(trz[k - 1], rows(zh), rows(zh), device(x, y, (zh + k) % 4, zl, core))

    total = g_small[0, pl.ds(pl.multiple_of(z * 8, 8), 8)]
    for k in range(1, 8):
        w.wait(tgz[k - 1], z_in.at[k - 1], partner)
    for k in range(7):
        total = total + z_in[k]
    g_last[...] = total
    ts = w.number()
    w.start(ts, g_last, g_swap, partner)

    for k in range(1, 4):
        w.wait(trz[k - 1], rows((zh + 4 - k) % 4), partner)
    spread = Spread(w, block, dto, da, db, lambda a, b, j: None)
    spread.begin()

    w.wait(ts, g_swap, partner)
    here, there = g_last[...], g_swap[...]
    left = jnp.where(core == 0, here, there)
    right = jnp.where(core == 0, there, here)
    e_ref[:, 0:COLS] = jnp.where(core == 0, left[0:4], left[4:8])
    e_ref[:, COLS:2 * COLS] = jnp.where(core == 0, right[0:4], right[4:8])
    spread.rest()
    w.drain()


def reduce_all(g, d):
    messages = 16 + 6 * 4 + 3 + 7 + 3 + 1 + 20
    e, r = pl.pallas_call(
        reduce_kernel,
        out_shape=(jax.ShapeDtypeStruct((4, 2 * COLS), F32), jax.ShapeDtypeStruct((4, 4, 64, COLS), WIRE)),
        in_specs=[pl.BlockSpec(memory_space=VMEM)] * 2,
        out_specs=[pl.BlockSpec(memory_space=VMEM)] * 2,
        scratch_shapes=[
            pltpu.SemaphoreType.DMA((messages,)),
            pltpu.SemaphoreType.DMA((messages,)),
            VMEM((4, 4, 64, COLS), F32),
            VMEM((4, 4, 64, COLS), F32),
            VMEM((6, 2, 64, COLS), WIRE),
            VMEM((6, 2, 64, COLS), WIRE),
            VMEM((6, 32, COLS), WIRE),
            VMEM((6, 32, COLS), WIRE),
            VMEM((4, 64, COLS), F32),
            VMEM((7, 8, COLS), F32),
            VMEM((8, COLS), F32),
            VMEM((8, COLS), F32),
            VMEM((6, 2, 64, COLS), WIRE),
            VMEM((6, 2, 64, COLS), WIRE),
            VMEM((6, 32, COLS), WIRE),
            VMEM((6, 32, COLS), WIRE),
            VMEM((4, 64, COLS), F32),
            VMEM((3, 16, COLS), F32),
        ],
        compiler_params=pltpu.CompilerParams(collective_id=1, has_side_effects=True, vmem_limit_bytes=48 << 20),
        name="reduce_all",
    )(g.reshape(2, 4, 4, 64, COLS), d.reshape(4, 4, 64, COLS))
    return e, r.astype(F32).reshape(1024, COLS)


def compute_kernel(cols_ref, rows_ref, phases_ref, table_ref, g_ref, d_ref,
                   parts, cos_ref, sin_ref, word_ref, query_ref, weight_ref, back_ref, turn_ref, square_ref):
    rows_n, listed_n = 512, 32
    lanes = lax.broadcasted_iota(jnp.int32, (1, 1024), 1)
    lane = lax.broadcasted_iota(jnp.int32, (1, 128), 1)
    step = 128

    def dot(a, b):
        return jnp.dot(a, b, preferred_element_type=F32)

    def dot_nt(a, b):
        return lax.dot_general(a, b, (((1,), (1,)), ((), ())), preferred_element_type=F32)

    def dot_tn(a, b):
        return lax.dot_general(a, b, (((0,), (0,)), ((), ())), preferred_element_type=F32)

    def split(i, _):
        at = pl.ds(pl.multiple_of(i * step, step), step)
        p = phases_ref[at]
        for k in range(3):
            q = p.astype(BF16)
            parts[k, at] = q
            p = p - q.astype(F32)
        t = table_ref[at].astype(F32)
        s = jnp.sum(t * t, axis=1, keepdims=True)
        square_ref[i] = jnp.transpose(jnp.broadcast_to(s, (step, 128)))[0:8]
        return 0

    lax.fori_loop(0, 8, split, 0)

    def prepare(i, _):
        at = pl.ds(pl.multiple_of(i * step, step), step)
        ids = cols_ref[at]
        hot = (ids[:, 1:2] == lanes).astype(F32).astype(BF16)
        angle = dot(hot, parts[0]) + dot(hot, parts[1]) + dot(hot, parts[2])
        t = angle * angle
        c = horner(COS, t)
        s = angle * horner(SIN, t)
        cos_ref[at] = c
        sin_ref[at] = s
        low = ids & 127
        bit = jnp.left_shift(jnp.int32(1), jnp.right_shift(ids, 7))
        word = jnp.zeros((step, 128), jnp.int32)
        for j in range(3, 3 + listed_n):
            word = word | jnp.where(low[:, j:j + 1] == lane, bit[:, j:j + 1], 0)
        keep = jnp.where(low[:, 2:3] == lane, bit[:, 2:3], 0)
        word_ref[at] = (word & ~keep) | jnp.left_shift(keep, 8)
        return 0

    lax.fori_loop(0, rows_n // step, prepare, 0)

    def main(i, _):
        at = pl.ds(pl.multiple_of(i * step, step), step)
        ids = cols_ref[at]
        hot = (ids[:, 0:1] == lanes).astype(F32).astype(BF16)
        head = dot(hot, table_ref[...])
        c, s = cos_ref[at], sin_ref[at]
        hr, hm = head[:, :512], head[:, 512:]
        qr = hr * c - hm * s
        qm = hr * s + hm * c
        query = jnp.concatenate([qr, qm], axis=1).astype(BF16)
        query_ref[at] = query
        rounded = query.astype(F32)
        query_sq = jnp.sum(rounded * rounded, axis=1, keepdims=True)
        cross = dot_nt(query, table_ref[...])
        word = word_ref[at]
        scores, hidden = [], []
        top = None
        for k in range(8):
            sc = 2.0 * cross[:, k * 128:(k + 1) * 128] - query_sq - square_ref[k, 0:1]
            hide = (word & (1 << k)) != 0
            scores.append(sc)
            hidden.append(hide)
            seen = jnp.where(hide, -jnp.inf, sc)
            top = seen if top is None else jnp.maximum(top, seen)
        top = jnp.max(top, axis=1, keepdims=True)
        raws = []
        for k in range(8):
            raws.append(jnp.where(hidden[k], 0.0, jnp.exp(scores[k] - top)))
        total = raws[0]
        for k in range(1, 8):
            total = total + raws[k]
        scale = 1.0 / jnp.sum(total, axis=1, keepdims=True)
        weights = []
        for k in range(8):
            hit = (word & (256 << k)) != 0
            wk = (raws[k] * scale - jnp.where(hit, 1.0, 0.0)).astype(BF16)
            weights.append(wk)
            weight_ref[k, at] = wk
        grad = 2.0 * dot(jnp.concatenate(weights, axis=1), table_ref[...])
        gr, gm = grad[:, :512], grad[:, 512:]
        back_ref[at] = jnp.concatenate([gr * c + gm * s, gm * c - gr * s], axis=1).astype(BF16)
        turn = qr * gm - qm * gr
        high = turn.astype(BF16)
        turn_ref[0, at] = high
        turn_ref[1, at] = (turn - high.astype(F32)).astype(BF16)
        return 0

    lax.fori_loop(0, rows_n // step, main, 0)

    ones = jnp.ones((rows_n, 128), BF16)

    def finish(i, _):
        at = pl.ds(pl.multiple_of(i * step, step), step)
        key = lax.broadcasted_iota(jnp.int32, (step, 1), 0) + i * step
        wk = weight_ref[i]
        cross = dot_tn(wk, query_ref[...])
        counts = dot_tn(wk, ones)
        hot = (rows_ref[0:1] == key).astype(F32).astype(BF16)
        back = dot(hot, back_ref[...])
        t = table_ref[at].astype(F32)
        many = jnp.concatenate([counts] * 8, axis=1)
        out = 2.0 * (cross - many * t) + back
        g_ref[0, at] = out[:, :512]
        g_ref[1, at] = out[:, 512:]
        hot = (rows_ref[1:2] == key).astype(F32).astype(BF16)
        d_ref[at] = dot(hot, turn_ref[0]) + dot(hot, turn_ref[1])
        return 0

    lax.fori_loop(0, 8, finish, 0)


def compute(cols, rows, phases, table):
    return pl.pallas_call(
        compute_kernel,
        out_shape=(jax.ShapeDtypeStruct((2, 1024, COLS), F32), jax.ShapeDtypeStruct((1024, COLS), F32)),
        in_specs=[pl.BlockSpec(memory_space=VMEM)] * 4,
        out_specs=[pl.BlockSpec(memory_space=VMEM)] * 2,
        scratch_shapes=[
            VMEM((3, 1024, 512), BF16),
            VMEM((512, 512), F32),
            VMEM((512, 512), F32),
            VMEM((512, 128), jnp.int32),
            VMEM((512, 1024), BF16),
            VMEM((8, 512, 128), BF16),
            VMEM((512, 1024), BF16),
            VMEM((2, 512, 512), BF16),
            VMEM((8, 8, 128), F32),
        ],
        compiler_params=pltpu.CompilerParams(vmem_limit_bytes=56 << 20),
        name="compute",
    )(cols, rows, phases, table)


def local(entity_table, phases, head_owner, head_row, relation, tail_ids, known_tails):
    heads = head_owner[:, 0] * 4 + head_row
    cols = jnp.concatenate([heads[:, None], relation[:, None], tail_ids[:, None], known_tails], axis=1)
    rows = jnp.stack([heads, relation])
    table = gather_table(entity_table)
    g, d = compute(cols, rows, phases, table)
    return reduce_all(g, d)


def solution(mesh):
    in_specs = (
        P("ent", None),
        P("rel", None),
        P(("ent", "rel"), None),
        P(("ent", "rel")),
        P(("ent", "rel")),
        P(("ent", "rel")),
        P(("ent", "rel"), None),
    )
    out_specs = (P(("ent", "rel"), None), P("rel", None))
    return jax.shard_map(local, mesh=mesh, in_specs=in_specs, out_specs=out_specs, check_vma=False)
```

time: 1180 us -> 119 us (0.10)
  the two profiles are of different devices: /device:TPU:32 before, /device:TPU:2 now
where the time goes in v1:
time: 119 us; the launch traced here: 118 us
  Pallas kernels  109 us (92%)
  other arithmetic  5.2 us (4%)
  local copies, waits for them, and re-layouts  3.05 us (3%)
    pallas_call x1, Pallas kernels, reduce_all(): pl.pallas_call(reduce_kernel, out_shape=(jax.ShapeDtypeStruct((4, 2 * COL...  53.5 us
    pallas_call x1, Pallas kernels, gather_table(): pl.pallas_call(gather_kernel, out_shape=jax.ShapeDtypeStruct((4, 4, 64, 2...  29.8 us
    pallas_call x1, Pallas kernels, compute(): pl.pallas_call(compute_kernel, out_shape=(jax.ShapeDtypeStruct((2, 1024,...  26.1 us

profile of v1, /device:TPU:2, one launch (start us, length us, event | category | flops | bytes accessed | tf_op | source)
XLA Modules:
  0.0 118.4 jit_solution(1231089455535983204)
XLA Ops:
  0.6 0.7 broadcast_multiply_fusion
  1.3 0.7 add.3
  2.0 1.3 %pad_add_fusion.1.rows_ref = s32[2,512]{1,0:T(2,128)} fusion(s32[1,512]{1,0:T(1,128)} %bitcast.17, s32[1,512]{1,0:T(1,128)S(1)} %bitcast.15), kind=kLoop, calls=%fused_computation.2 | loop fusion | flops 1024 | bytes 8192 | tf_op jit(solution)/shard_map/stack | solution.py:589
  3.3 0.9 pad_add_fusion
  4.2 0.9 copy.14.cols_ref
  5.0 29.8 %gather_table.1 = bf16[4,4,64,1024]{3,2,1,0:T(8,128)(2,1)} custom-call(bf16[16,1024]{1,0:T(8,128)(2,1)} %entity_ref.1), custom_call_target="tpu_custom_call" | custom-call | tf_op jit(solution)/shard_map/gather_table/pallas_call | solution.py:251
  34.9 26.1 %compute.1 = (f32[2,1024,512]{2,1,0:T(8,128)}, f32[1024,512]{1,0:T(8,128)}) custom-call(s32[512,35]{1,0:T(8,128)} %copy.14.cols_ref, s32[2,512]{1,0:T(2,128)} %pad_add_fusion.1.rows_ref, f32[1024,512]{1,0:T(8,128)} %phases_ref.1, bf16[1024,1024]{1,0:T(8,128)(2,1)} %bitcast.13), custom_call_target="tpu_custom_call" | custom-call | tf_op jit(solution)/shard_map/compute/pallas_call | solution.py:565
  61.0 0.0 copy-start
  61.0 1.6 %copy-done = f32[1024,512]{1,0:T(8,128)S(1)} copy-done((f32[1024,512]{1,0:T(8,128)S(1)}, f32[1024,512]{1,0:T(8,128)}, u32[]{:S(2)}) %copy-start) | copy-done | bytes 2097176
  62.6 53.5 %reduce_all.1 = (f32[4,1024]{1,0:T(4,128)S(1)}, bf16[4,4,64,512]{3,2,1,0:T(8,128)(2,1)S(1)}) custom-call(f32[2,4,4,64,512]{4,3,2,1,0:T(8,128)} %bitcast.14, f32[4,4,64,512]{3,2,1,0:T(8,128)S(1)} %bitcast.12), custom_call_target="tpu_custom_call" | custom-call | tf_op jit(solution)/shard_map/reduce_all/pallas_call | solution.py:411
  116.1 1.7 %bitcast_convert_fusion = f32[1024,512]{1,0:T(8,128)} fusion(bf16[4,4,64,512]{3,2,1,0:T(8,128)(2,1)S(1)} %get-tuple-element.9), kind=kLoop, calls=%fused_computation | loop fusion | flops 524288 | bytes 3145728 | tf_op jit(solution)/shard_map/reshape | solution.py:439
  117.8 0.6 copy.16
Async XLA Ops:
  61.0 1.6 %copy-start = (f32[1024,512]{1,0:T(8,128)S(1)}, f32[1024,512]{1,0:T(8,128)}, u32[]{:S(2)}) copy-start(f32[1024,512]{1,0:T(8,128)} %get-tuple-element.7) | copy-start | bytes 6291460

commit v2 on v0

v2 whole, which is shorter than its diff:
```python
import functools

import jax
import jax.numpy as jnp
from jax import lax
from jax.experimental import pallas as pl
from jax.experimental.pallas import tpu as pltpu
from jax.sharding import PartitionSpec as P

MESH = pl.DeviceIdType.MESH
VMEM = pltpu.VMEM
F32 = jnp.float32
BF16 = jnp.bfloat16
WIRE = jnp.bfloat16
COLS = 512

SIN = (0.9999999999932018, -0.16666666657817392, 0.008333333144447052, -0.00019841254471923497,
       2.7556704311932283e-06, -2.5038717712098566e-08, 1.5896746642760318e-10, -6.610935072102146e-13)
COS = (0.9999999999990714, -0.4999999999846839, 0.041666666625163704, -0.0013888888455803566,
       2.480156464708791e-05, -2.755665269895137e-07, 2.0865211281170485e-09, -1.1353643820753535e-11,
       4.131574377242709e-14)


def horner(coefficients, t):
    value = jnp.full_like(t, coefficients[-1])
    for c in coefficients[-2::-1]:
        value = value * t + c
    return value


def place():
    e = lax.axis_index("ent")
    r = lax.axis_index("rel")
    return e // 16, (e // 4) % 4, e % 4, r // 2, r % 2


def device(x, y, zh, zl, core):
    return {"ent": x * 16 + y * 4 + zh, "rel": zl * 2 + core}


class Wire:
    def __init__(self, send, recv):
        self.send, self.recv = send, recv
        self.count = 0
        self.open = []

    def number(self):
        self.count += 1
        return self.count - 1

    def start(self, t, src, dst, to):
        copy = pltpu.make_async_remote_copy(
            src_ref=src, dst_ref=dst, send_sem=self.send.at[t], recv_sem=self.recv.at[t],
            device_id=to, device_id_type=MESH)
        copy.start()
        self.open.append(copy)

    def wait(self, t, dst, to):
        pltpu.make_async_remote_copy(
            src_ref=dst, dst_ref=dst, send_sem=self.send.at[t], recv_sem=self.recv.at[t],
            device_id=to, device_id_type=MESH).wait_recv()

    def drain(self):
        for copy in self.open:
            copy.wait_send()
        self.open = []


def greet(x, y, zh, zl, core):
    barrier = pltpu.get_barrier_semaphore()
    z = zh * 2 + zl
    peers = [device(x, y, zh, zl, 1 - core)]
    for d in (1, 2, 3):
        peers.append(device((x + d) % 4, y, zh, zl, core))
        peers.append(device(x, (y + d) % 4, zh, zl, core))
    for d in range(1, 8):
        zz = (z + d) % 8
        peers.append(device(x, y, zz // 2, zz % 2, core))
    for peer in peers:
        pl.semaphore_signal(barrier, inc=1, device_id=peer, device_id_type=MESH)
    pl.semaphore_wait(barrier, len(peers))


class Spread:
    def __init__(self, wire, block, to, a0, b0, have):
        self.w, self.block, self.to, self.a0, self.b0, self.have = wire, block, to, a0, b0, have
        self.tb = [wire.number() for _ in range(3)]
        self.ta = [[wire.number() for _ in range(3)] for _ in range(4)]

    def got(self, j):
        b = (self.b0 + j) % 4
        blk = self.block(self.a0, b)
        for k in (2, 1, 3):
            self.w.start(self.ta[j][k - 1], blk, blk, self.to((self.a0 + k) % 4, self.b0))
        self.have(self.a0, b, j)

    def begin(self):
        blk = self.block(self.a0, self.b0)
        for k in (2, 1, 3):
            self.w.start(self.tb[k - 1], blk, blk, self.to(self.a0, (self.b0 + k) % 4))
        self.got(0)

    def along_b(self):
        for k in (1, 3, 2):
            j = 4 - k
            b = (self.b0 + j) % 4
            self.w.wait(self.tb[k - 1], self.block(self.a0, b), self.to(self.a0, b))
            self.got(j)

    def along_a(self, j):
        b = (self.b0 + j) % 4
        for k in (1, 3, 2):
            a = (self.a0 + 4 - k) % 4
            self.w.wait(self.ta[j][k - 1], self.block(a, b), self.to(a, self.b0))
            self.have(a, b, 4 * k + j)


class Collect:
    def __init__(self, wire, piece, to, m, out, inn):
        self.w, self.piece, self.to, self.m, self.out, self.inn = wire, piece, to, m, out, inn
        self.t = [wire.number() for _ in range(3)]

    def begin(self):
        for k in (2, 1, 3):
            c = (self.m + k) % 4
            self.out[k - 1] = self.piece(c).astype(self.out.dtype)
            self.w.start(self.t[k - 1], self.out.at[k - 1], self.inn.at[k - 1], self.to(c))

    def end(self):
        for k in (1, 3, 2):
            self.w.wait(self.t[k - 1], self.inn.at[k - 1], self.to((self.m + 4 - k) % 4))
        inn = self.inn
        return self.piece(self.m) + ((inn[0].astype(F32) + inn[2].astype(F32)) + inn[1].astype(F32))


def dot(a, b):
    return jnp.dot(a, b, preferred_element_type=F32)


def dot_nt(a, b):
    return lax.dot_general(a, b, (((1,), (1,)), ((), ())), preferred_element_type=F32)


def dot_tn(a, b):
    return lax.dot_general(a, b, (((0,), (0,)), ((), ())), preferred_element_type=F32)


def span(i, n):
    return pl.ds(pl.multiple_of(i * n, n), n)


STEP = 128
TRIPLES = 512
LISTED = 32


def step_kernel(known_ref, owner_ref, place_ref, relation_ref, tail_ref, phases_hbm, entity_ref, e_ref, r_ref,
                send, recv, local_sem, phases_sem,
                phases_ref, parts, cos_ref, sin_ref, word_ref, head_ref, table_ref, square_ref,
                query_ref, weight_ref, back_ref, turn_ref, g_ref, pair, d_ref,
                g_acc, g_out, g_in, h_out, h_in, g_small, z_in, g_last, g_swap,
                d_out, d_in, f_out, f_in, d_small, d_zin):
    x, y, zh, zl, core = place()
    z = zh * 2 + zl
    other = 1 - core
    z_sign = 2 * zl - 1
    mine = span(core, COLS)
    theirs = span(other, COLS)
    partner = device(x, y, zh, zl, other)
    w = Wire(send, recv)

    fetch = pltpu.make_async_copy(phases_hbm, phases_ref, phases_sem)
    fetch.start()
    ga, gb = x * other + y * core, y * other + x * core
    da, db = gb, ga

    def gxy(a, b):
        return a * other + b * core, b * other + a * core

    def dxy(a, b):
        return b * other + a * core, a * other + b * core

    def gspan(a, b):
        px, py = gxy(a, b)
        return span(px * 4 + py, 64)

    def dspan(a, b):
        px, py = dxy(a, b)
        return span(px * 4 + py, 64)

    def gto(a, b):
        px, py = gxy(a, b)
        return device(px, py, zh, zl, core)

    def dto(a, b):
        px, py = dxy(a, b)
        return device(px, py, zh, zl, core)

    greet(x, y, zh, zl, core)

    tp = [w.number() for _ in range(16)]
    tz = [w.number() for _ in range(3)]

    def block(a, b):
        return table_ref.at[gspan(a, b), mine]

    def rows(k):
        return table_ref.at[pl.ds(pl.multiple_of((x * 4 + y) * 64 + k * 16, 16), 16), mine]

    own = pltpu.make_async_copy(entity_ref.at[:, mine], rows(zh), local_sem)
    own.start()
    z_to = [((zh + z_sign + 4) % 4, 1 - zl), ((zh + z_sign + 4) % 4, zl), ((zh + 2) % 4, 1 - zl)]
    for t, (h, l) in zip(tz, z_to):
        w.start(t, entity_ref.at[:, mine], rows(zh), device(x, y, h, l, core))

    fetch.wait()

    def split(i, _):
        at = span(i, STEP)
        p = phases_ref[at]
        for k in range(3):
            q = p.astype(BF16)
            parts[k, at] = q
            p = p - q.astype(F32)
        return 0

    lax.fori_loop(0, 8, split, 0)

    lane = lax.broadcasted_iota(jnp.int32, (1, STEP), 1)

    def down(row):
        return jnp.transpose(jnp.broadcast_to(row, (STEP, STEP)))

    def hot_rows(col):
        return jnp.concatenate([(col == lane + 128 * k).astype(F32).astype(BF16) for k in range(8)], axis=1)

    def prepare(i, _):
        at = span(i, STEP)
        head_ref[at] = down(owner_ref[:, at] * 4 + place_ref[:, at])
        hot = hot_rows(down(relation_ref[:, at]))
        angle = dot(hot, parts[0]) + dot(hot, parts[1]) + dot(hot, parts[2])
        t = angle * angle
        cos_ref[at] = horner(COS, t)
        sin_ref[at] = angle * horner(SIN, t)
        ids = jnp.transpose(known_ref[:, at])
        low = ids & 127
        bit = jnp.left_shift(jnp.int32(1), jnp.right_shift(ids, 7))
        word = jnp.zeros((STEP, STEP), jnp.int32)
        for j in range(LISTED):
            word = word | jnp.where(low[:, j:j + 1] == lane, bit[:, j:j + 1], 0)
        tail = down(tail_ref[:, at])
        keep = jnp.where((tail & 127) == lane, jnp.left_shift(jnp.int32(1), jnp.right_shift(tail, 7)), 0)
        word_ref[at] = (word & ~keep) | jnp.left_shift(keep, 8)
        return 0

    lax.fori_loop(0, 1, prepare, 0)
    z_from = [(zh + z_sign + 4) % 4, (zh - z_sign + 4) % 4, (zh + 2) % 4]
    for t, h in zip(tz, z_from):
        w.wait(t, rows(h), partner)
    own.wait()

    def have(a, b, j):
        w.start(tp[j], block(a, b), block(a, b), partner)

    spread = Spread(w, block, gto, ga, gb, have)
    spread.begin()
    lax.fori_loop(1, 2, prepare, 0)
    spread.along_b()
    lax.fori_loop(2, 4, prepare, 0)
    for j in (0, 3, 1, 2):
        spread.along_a(j)
    for j in range(16):
        w.wait(tp[j], table_ref.at[pl.ds(0, 64), theirs], partner)

    def squares(i, _):
        t = table_ref[span(i, STEP)].astype(F32)
        s = jnp.sum(t * t, axis=1, keepdims=True)
        square_ref[i] = jnp.transpose(jnp.broadcast_to(s, (STEP, STEP)))[0:8]
        return 0

    lax.fori_loop(0, 8, squares, 0)

    def main(i, _):
        at = span(i, STEP)
        head = dot(hot_rows(head_ref[at]), table_ref[...])
        c, s = cos_ref[at], sin_ref[at]
        hr, hm = head[:, :COLS], head[:, COLS:]
        qr = hr * c - hm * s
        qm = hr * s + hm * c
        query = jnp.concatenate([qr, qm], axis=1).astype(BF16)
        query_ref[at] = query
        rounded = query.astype(F32)
        query_sq = jnp.sum(rounded * rounded, axis=1, keepdims=True)
        cross = dot_nt(query, table_ref[...])
        word = word_ref[at]
        scores, hidden = [], []
        top = None
        for k in range(8):
            sc = 2.0 * cross[:, k * 128:(k + 1) * 128] - query_sq - square_ref[k, 0:1]
            hide = (word & (1 << k)) != 0
            scores.append(sc)
            hidden.append(hide)
            seen = jnp.where(hide, -jnp.inf, sc)
            top = seen if top is None else jnp.maximum(top, seen)
        top = jnp.max(top, axis=1, keepdims=True)
        raws = []
        for k in range(8):
            raws.append(jnp.where(hidden[k], 0.0, jnp.exp(scores[k] - top)))
        total = raws[0]
        for k in range(1, 8):
            total = total + raws[k]
        scale = 1.0 / jnp.sum(total, axis=1, keepdims=True)
        weights = []
        for k in range(8):
            hit = (word & (256 << k)) != 0
            wk = (raws[k] * scale - jnp.where(hit, 1.0, 0.0)).astype(BF16)
            weights.append(wk)
            weight_ref[k, at] = wk
        grad = 2.0 * dot(jnp.concatenate(weights, axis=1), table_ref[...])
        gr, gm = grad[:, :COLS], grad[:, COLS:]
        back_ref[at] = jnp.concatenate([gr * c + gm * s, gm * c - gr * s], axis=1).astype(BF16)
        turn = qr * gm - qm * gr
        high = turn.astype(BF16)
        turn_ref[0, at] = high
        turn_ref[1, at] = (turn - high.astype(F32)).astype(BF16)
        return 0

    lax.fori_loop(0, TRIPLES // STEP, main, 0)

    def key(i):
        return lax.broadcasted_iota(jnp.int32, (STEP, 1), 0) + i * STEP

    def relations(i, _):
        hot = (relation_ref[...] == key(i)).astype(F32).astype(BF16)
        d_ref[span(i, STEP)] = dot(hot, turn_ref[0]) + dot(hot, turn_ref[1])
        return 0

    lax.fori_loop(0, 8, relations, 0)

    def d_piece(c):
        return jnp.concatenate([d_ref[dspan(c, b)][None] for b in range(4)], axis=0)

    d_first = Collect(w, d_piece, lambda a: dto(a, db), da, d_out, d_in)
    d_first.begin()

    ones = jnp.ones((TRIPLES, 128), BF16)
    heads = owner_ref[...] * 4 + place_ref[...]

    def dense(i):
        at = span(i, STEP)
        wk = weight_ref[i]
        cross = dot_tn(wk, query_ref[...])
        counts = dot_tn(wk, ones)
        hot = (heads == key(i)).astype(F32).astype(BF16)
        back = dot(hot, back_ref[...])
        t = table_ref[at].astype(F32)
        many = jnp.concatenate([counts] * 8, axis=1)
        out = 2.0 * (cross - many * t) + back
        g_ref[0, at] = out[:, :COLS]
        g_ref[1, at] = out[:, COLS:]

    tg = [w.number() for _ in range(8)]

    def turn_of(n):
        return (x * 2 + 4 + n) % 8

    for n in range(8):
        i = turn_of(n)
        dense(i)
        w.start(tg[n], g_ref.at[other, span(i, STEP)], pair.at[span(i, STEP)], partner)

    def add_pair(n):
        i = turn_of(n)
        w.wait(tg[n], pair.at[span(i, STEP)], partner)
        g_acc[span(i, STEP)] = g_ref[core, span(i, STEP)] + pair[span(i, STEP)]

    for n in range(8):
        add_pair(n)

    def g_piece(c):
        return jnp.concatenate([g_acc[gspan(c, b)][None] for b in range(4)], axis=0)

    g_first = Collect(w, g_piece, lambda a: gto(a, gb), ga, g_out, g_in)
    g_first.begin()

    d_small[...] = d_first.end()
    d_second = Collect(w, lambda c: d_small[c], lambda b: dto(da, b), db, f_out, f_in)
    d_second.begin()

    tdz = [w.number() for _ in range(3)]
    tgz = [w.number() for _ in range(7)]
    trz = [w.number() for _ in range(3)]
    ts = w.number()
    d_small[0] = d_second.end()
    for k in (2, 1, 3):
        hh = (zh + k) % 4
        w.start(tdz[k - 1], d_small.at[0, span(hh, 16)], d_zin.at[k - 1], device(x, y, hh, zl, core))

    g_small[...] = g_first.end()
    g_second = Collect(w, lambda c: g_small[c], lambda b: gto(ga, b), gb, h_out, h_in)
    g_second.begin()

    def r_block(a, b):
        return r_ref.at[dspan(a, b)]

    def r_rows(k):
        return r_ref.at[pl.ds(pl.multiple_of((x * 4 + y) * 64 + k * 16, 16), 16)]

    for k in (1, 3, 2):
        w.wait(tdz[k - 1], d_zin.at[k - 1], partner)
    total = d_small[0, span(zh, 16)] + ((d_zin[0] + d_zin[1]) + d_zin[2])
    r_rows(zh)[...] = total.astype(r_ref.dtype)
    for k in (2, 1, 3):
        w.start(trz[k - 1], r_rows(zh), r_rows(zh), device(x, y, (zh + k) % 4, zl, core))

    g_small[0] = g_second.end()
    for k in (4, 3, 5, 2, 6, 1, 7):
        zz = (z + k) % 8
        w.start(tgz[k - 1], g_small.at[0, span(zz, 8)], z_in.at[k - 1], device(x, y, zz // 2, zz % 2, core))

    for k in (1, 3, 2):
        w.wait(trz[k - 1], r_rows((zh + 4 - k) % 4), partner)
    back = Spread(w, r_block, dto, da, db, lambda a, b, j: None)
    back.begin()

    total = g_small[0, span(z, 8)]
    for k in range(1, 8):
        w.wait(tgz[k - 1], z_in.at[k - 1], partner)
    for k in range(7):
        total = total + z_in[k]
    g_last[...] = total
    w.start(ts, g_last, g_swap, partner)

    back.along_b()
    w.wait(ts, g_swap, partner)
    here, there = g_last[...], g_swap[...]
    left = jnp.where(core == 0, here, there)
    right = jnp.where(core == 0, there, here)
    e_ref[:, 0:COLS] = jnp.where(core == 0, left[0:4], left[4:8])
    e_ref[:, COLS:2 * COLS] = jnp.where(core == 0, right[0:4], right[4:8])
    for j in (0, 3, 1, 2):
        back.along_a(j)
    w.drain()


def local(entity_table, phases, head_owner, head_row, relation, tail_ids, known_tails):
    messages = 16 + 3 + 15 + 12 + 8 + 3 + 7 + 3 + 1 + 15
    here = pl.BlockSpec(memory_space=VMEM)
    e, r = pl.pallas_call(
        step_kernel,
        out_shape=(jax.ShapeDtypeStruct((4, 2 * COLS), F32), jax.ShapeDtypeStruct((1024, COLS), WIRE)),
        in_specs=[here] * 5 + [pl.BlockSpec(memory_space=pl.ANY), here],
        out_specs=[here, here],
        scratch_shapes=[
            pltpu.SemaphoreType.DMA((messages,)),
            pltpu.SemaphoreType.DMA((messages,)),
            pltpu.SemaphoreType.DMA,
            pltpu.SemaphoreType.DMA,
            VMEM((1024, COLS), F32),
            VMEM((3, 1024, COLS), BF16),
            VMEM((TRIPLES, COLS), F32),
            VMEM((TRIPLES, COLS), F32),
            VMEM((TRIPLES, STEP), jnp.int32),
            VMEM((TRIPLES, STEP), jnp.int32),
            VMEM((1024, 2 * COLS), BF16),
            VMEM((8, 8, STEP), F32),
            VMEM((TRIPLES, 2 * COLS), BF16),
            VMEM((8, TRIPLES, STEP), BF16),
            VMEM((TRIPLES, 2 * COLS), BF16),
            VMEM((2, TRIPLES, COLS), BF16),
            VMEM((2, 1024, COLS), F32),
            VMEM((1024, COLS), F32),
            VMEM((1024, COLS), F32),
            VMEM((1024, COLS), F32),
            VMEM((3, 4, 64, COLS), WIRE),
            VMEM((3, 4, 64, COLS), WIRE),
            VMEM((3, 64, COLS), WIRE),
            VMEM((3, 64, COLS), WIRE),
            VMEM((4, 64, COLS), F32),
            VMEM((7, 8, COLS), F32),
            VMEM((8, COLS), F32),
            VMEM((8, COLS), F32),
            VMEM((3, 4, 64, COLS), WIRE),
            VMEM((3, 4, 64, COLS), WIRE),
            VMEM((3, 64, COLS), WIRE),
            VMEM((3, 64, COLS), WIRE),
            VMEM((4, 64, COLS), F32),
            VMEM((3, 16, COLS), F32),
        ],
        compiler_params=pltpu.CompilerParams(collective_id=0, has_side_effects=True, vmem_limit_bytes=58 << 20),
        name="step",
    )(known_tails.T, head_owner.reshape(1, TRIPLES), head_row.reshape(1, TRIPLES), relation.reshape(1, TRIPLES),
      tail_ids.reshape(1, TRIPLES), phases, entity_table)
    return e, r.astype(F32)


def solution(mesh):
    in_specs = (
        P("ent", None),
        P("rel", None),
        P(("ent", "rel"), None),
        P(("ent", "rel")),
        P(("ent", "rel")),
        P(("ent", "rel")),
        P(("ent", "rel"), None),
    )
    out_specs = (P(("ent", "rel"), None), P("rel", None))
    return jax.shard_map(local, mesh=mesh, in_specs=in_specs, out_specs=out_specs, check_vma=False)
```

time: 1180 us -> 84.4 us (0.07)
  the two profiles are of different devices: /device:TPU:32 before, /device:TPU:8 now
where the time goes in v2:
time: 84.4 us; the launch traced here: 84.2 us
  Pallas kernels  80.1 us (95%)
  other arithmetic  2.84 us (3%)
    pallas_call x1, Pallas kernels, local(): pl.pallas_call(step_kernel, out_shape=(jax.ShapeDtypeStruct((4, 2 * COLS)...  80.1 us
    convert_element_type x1, other arithmetic, local(): return (e, r.astype(F32))  2.84 us

profile of v2, /device:TPU:8, one launch (start us, length us, event | category | flops | bytes accessed | tf_op | source)
XLA Modules:
  0.0 84.2 jit_solution(12405849457693884502)
XLA Ops:
  0.6 80.1 %step.1 = (f32[4,1024]{1,0:T(4,128)}, bf16[1024,512]{1,0:T(8,128)(2,1)}) custom-call(s32[32,512]{1,0:T(8,128)} %bitcast.5, s32[1,512]{1,0:T(1,128)} %bitcast.6, s32[1,512]{1,0:T(1,128)} %bitcast.7, s32[1,512]{1,0:T(1,128)} %bitcast.8, s32[1,512]{1,0:T(1,128)} %bitcast.9, f32[1024,512]{1,0:T(8,128)} %phases_hbm.1, bf16[16,1024]{1,0:T(8,128)(2,1)} %entity_ref.1), custom_call_target="tpu_custom_call" | custom-call | tf_op jit(solution)/shard_map/step/pallas_call | solution.py:449
  80.8 0.0 copy-start
  80.8 2.8 %convert_element_type.3 = f32[1024,512]{1,0:T(8,128)} convert(bf16[1024,512]{1,0:T(8,128)(2,1)} %get-tuple-element.5) | non-fusion elementwise | flops 524288 | bytes 3145728 | tf_op jit(solution)/shard_map/convert_element_type | solution.py:494
  83.6 0.0 copy-done
  83.6 0.6 copy.10
Async XLA Ops:
  80.8 2.9 %copy-start = (f32[4,1024]{1,0:T(4,128)S(1)}, f32[4,1024]{1,0:T(4,128)}, u32[]{:S(2)}) copy-start(f32[4,1024]{1,0:T(4,128)} %get-tuple-element.8) | copy-start | bytes 49156

commit v3 on v2

v3 whole, which is shorter than its diff:
```python
import functools

import jax
import jax.numpy as jnp
from jax import lax
from jax.experimental import pallas as pl
from jax.experimental.pallas import tpu as pltpu
from jax.sharding import PartitionSpec as P

MESH = pl.DeviceIdType.MESH
VMEM = pltpu.VMEM
F32 = jnp.float32
BF16 = jnp.bfloat16
WIRE = jnp.bfloat16
COLS = 512

SIN = (0.9999999999932018, -0.16666666657817392, 0.008333333144447052, -0.00019841254471923497,
       2.7556704311932283e-06, -2.5038717712098566e-08, 1.5896746642760318e-10, -6.610935072102146e-13)
COS = (0.9999999999990714, -0.4999999999846839, 0.041666666625163704, -0.0013888888455803566,
       2.480156464708791e-05, -2.755665269895137e-07, 2.0865211281170485e-09, -1.1353643820753535e-11,
       4.131574377242709e-14)


def horner(coefficients, t):
    value = jnp.full_like(t, coefficients[-1])
    for c in coefficients[-2::-1]:
        value = value * t + c
    return value


def place():
    e = lax.axis_index("ent")
    r = lax.axis_index("rel")
    return e // 16, (e // 4) % 4, e % 4, r // 2, r % 2


def device(x, y, zh, zl, core):
    return {"ent": x * 16 + y * 4 + zh, "rel": zl * 2 + core}


class Wire:
    def __init__(self, send, recv):
        self.send, self.recv = send, recv
        self.count = 0
        self.open = []

    def number(self):
        self.count += 1
        return self.count - 1

    def start(self, t, src, dst, to):
        copy = pltpu.make_async_remote_copy(
            src_ref=src, dst_ref=dst, send_sem=self.send.at[t], recv_sem=self.recv.at[t],
            device_id=to, device_id_type=MESH)
        copy.start()
        self.open.append(copy)

    def wait(self, t, dst, to):
        pltpu.make_async_remote_copy(
            src_ref=dst, dst_ref=dst, send_sem=self.send.at[t], recv_sem=self.recv.at[t],
            device_id=to, device_id_type=MESH).wait_recv()

    def drain(self):
        for copy in self.open:
            copy.wait_send()
        self.open = []


def greet(x, y, zh, zl, core):
    barrier = pltpu.get_barrier_semaphore()
    z = zh * 2 + zl
    peers = [device(x, y, zh, zl, 1 - core)]
    for d in (1, 2, 3):
        peers.append(device((x + d) % 4, y, zh, zl, core))
        peers.append(device(x, (y + d) % 4, zh, zl, core))
    for d in range(1, 8):
        zz = (z + d) % 8
        peers.append(device(x, y, zz // 2, zz % 2, core))
    for peer in peers:
        pl.semaphore_signal(barrier, inc=1, device_id=peer, device_id_type=MESH)
    pl.semaphore_wait(barrier, len(peers))


class Spread:
    def __init__(self, wire, block, to, a0, b0, own, z_to, z_from):
        self.w, self.block, self.to, self.a0, self.b0 = wire, block, to, a0, b0
        self.z_to, self.ks = z_to, [own] + z_from
        self.tz = [wire.number() for _ in range(3)]
        self.tb = [[wire.number() for _ in range(3)] for _ in range(4)]
        self.ta = [[[wire.number() for _ in range(3)] for _ in range(4)] for _ in range(4)]

    def along(self, q, j):
        blk = self.block(self.a0, (self.b0 + j) % 4, self.ks[q])
        for k in (2, 1, 3):
            self.w.start(self.ta[q][j][k - 1], blk, blk, self.to((self.a0 + k) % 4, self.b0))

    def on(self, q):
        blk = self.block(self.a0, self.b0, self.ks[q])
        for k in (2, 1, 3):
            self.w.start(self.tb[q][k - 1], blk, blk, self.to(self.a0, (self.b0 + k) % 4))
        self.along(q, 0)

    def begin(self):
        blk = self.block(self.a0, self.b0, self.ks[0])
        for i in range(3):
            self.w.start(self.tz[i], blk, blk, self.z_to[i])
        self.on(0)

    def take_z(self, i):
        self.w.wait(self.tz[i], self.block(self.a0, self.b0, self.ks[1 + i]), self.z_to[i])
        self.on(1 + i)

    def take_b(self, q):
        for k in (1, 3, 2):
            j = 4 - k
            b = (self.b0 + j) % 4
            self.w.wait(self.tb[q][k - 1], self.block(self.a0, b, self.ks[q]), self.to(self.a0, b))
            self.along(q, j)

    def take_a(self, q, j):
        for k in (1, 3, 2):
            a = (self.a0 + 4 - k) % 4
            self.w.wait(self.ta[q][j][k - 1], self.block(a, (self.b0 + j) % 4, self.ks[q]), self.to(a, self.b0))


FAR = (2, 1, 3, 0)


class Chain:
    def __init__(self, wire, load, to, a0, b0, zh, bufs):
        self.w, self.load, self.to, self.a0, self.b0 = wire, load, to, a0, b0
        self.ks = [(zh + off) % 4 for off in FAR]
        self.out_a, self.in_a, self.small, self.out_b, self.in_b, self.last = bufs
        self.ta = [[wire.number() for _ in range(3)] for _ in range(4)]
        self.tb = [[wire.number() for _ in range(3)] for _ in range(4)]

    def piece(self, c, q):
        return jnp.concatenate([self.load(c, b, self.ks[q])[None] for b in range(4)], axis=0)

    def begin_a(self, q):
        for k in (2, 1, 3):
            c = (self.a0 + k) % 4
            self.out_a[k - 1, q] = self.piece(c, q).astype(self.out_a.dtype)
            self.w.start(self.ta[q][k - 1], self.out_a.at[k - 1, q], self.in_a.at[k - 1, q], self.to(c, self.b0))

    def turn_b(self, q):
        for k in (1, 3, 2):
            self.w.wait(self.ta[q][k - 1], self.in_a.at[k - 1, q], self.to((self.a0 + 4 - k) % 4, self.b0))
        near = self.in_a[0, q].astype(F32) + self.in_a[2, q].astype(F32)
        self.small[q] = self.piece(self.a0, q) + (near + self.in_a[1, q].astype(F32))
        for k in (2, 1, 3):
            c = (self.b0 + k) % 4
            self.out_b[k - 1, q] = self.small[q, c].astype(self.out_b.dtype)
            self.w.start(self.tb[q][k - 1], self.out_b.at[k - 1, q], self.in_b.at[k - 1, q], self.to(self.a0, c))

    def end_b(self, q):
        for k in (1, 3, 2):
            self.w.wait(self.tb[q][k - 1], self.in_b.at[k - 1, q], self.to(self.a0, (self.b0 + 4 - k) % 4))
        near = self.in_b[0, q].astype(F32) + self.in_b[2, q].astype(F32)
        self.last[q] = self.small[q, self.b0] + (near + self.in_b[1, q].astype(F32))


def dot(a, b):
    return jnp.dot(a, b, preferred_element_type=F32)


def dot_nt(a, b):
    return lax.dot_general(a, b, (((1,), (1,)), ((), ())), preferred_element_type=F32)


def dot_tn(a, b):
    return lax.dot_general(a, b, (((0,), (0,)), ((), ())), preferred_element_type=F32)


def span(i, n):
    return pl.ds(pl.multiple_of(i * n, n), n)


STEP = 128
MAIN = 256
DENSE = 256
TRIPLES = 512
LISTED = 32


def step_kernel(known_ref, owner_ref, place_ref, relation_ref, tail_ref, phases_hbm, entity_ref, e_ref, r_ref,
                send, recv, local_sem, phases_sem,
                phases_ref, parts, cos_ref, sin_ref, word_ref, head_ref, table_ref, square_ref,
                query_ref, weight_ref, back_ref, turn_ref, g_ref, pair, d_ref,
                ga_out, ga_in, g_small, gb_out, gb_in, g_sum, g_zin, g_last, g_swap,
                da_out, da_in, d_small, db_out, db_in, d_sum, d_zin):
    x, y, zh, zl, core = place()
    other = 1 - core
    z_sign = 2 * zl - 1
    mine = span(core, COLS)
    theirs = span(other, COLS)
    partner = device(x, y, zh, zl, other)
    w = Wire(send, recv)

    fetch = pltpu.make_async_copy(phases_hbm, phases_ref, phases_sem)
    fetch.start()
    ga, gb = x * other + y * core, y * other + x * core
    da, db = gb, ga

    def gxy(a, b):
        return a * other + b * core, b * other + a * core

    def dxy(a, b):
        return b * other + a * core, a * other + b * core

    def gspan(a, b):
        px, py = gxy(a, b)
        return span(px * 4 + py, 64)

    def dspan(a, b):
        px, py = dxy(a, b)
        return span(px * 4 + py, 64)

    def gto(a, b):
        px, py = gxy(a, b)
        return device(px, py, zh, zl, core)

    def dto(a, b):
        px, py = dxy(a, b)
        return device(px, py, zh, zl, core)

    greet(x, y, zh, zl, core)

    tp = [w.number() for _ in range(16)]

    def block(a, b, k):
        px, py = gxy(a, b)
        return table_ref.at[core, span((px * 4 + py) * 4 + k, 16)]

    z_to = [device(x, y, (zh + z_sign + 4) % 4, 1 - zl, core), device(x, y, (zh + z_sign + 4) % 4, zl, core),
            device(x, y, (zh + 2) % 4, 1 - zl, core)]
    z_from = [(zh + z_sign + 4) % 4, (zh - z_sign + 4) % 4, (zh + 2) % 4]
    own = pltpu.make_async_copy(entity_ref.at[:, mine], block(ga, gb, zh), local_sem)
    own.start()
    own.wait()
    spread = Spread(w, block, gto, ga, gb, zh, z_to, z_from)
    spread.begin()

    def push(i, a, b):
        part = table_ref.at[core, gspan(a, b)]
        w.start(tp[i], part, part, partner)

    fetch.wait()

    def split(i, _):
        at = span(i, STEP)
        p = phases_ref[at]
        for k in range(3):
            q = p.astype(BF16)
            parts[k, at] = q
            p = p - q.astype(F32)
        return 0

    lax.fori_loop(0, 8, split, 0)

    lane = lax.broadcasted_iota(jnp.int32, (1, STEP), 1)

    def down(row):
        return jnp.transpose(jnp.broadcast_to(row, (STEP, STEP)))

    def hot_rows(col):
        return jnp.concatenate([(col == lane + 128 * k).astype(F32).astype(BF16) for k in range(8)], axis=1)

    def prepare(i, _):
        at = span(i, STEP)
        head_ref[at] = down(owner_ref[:, at] * 4 + place_ref[:, at])
        hot = hot_rows(down(relation_ref[:, at]))
        angle = dot(hot, parts[0]) + dot(hot, parts[1]) + dot(hot, parts[2])
        t = angle * angle
        cos_ref[at] = horner(COS, t)
        sin_ref[at] = angle * horner(SIN, t)
        ids = jnp.transpose(known_ref[:, at])
        low = ids & 127
        bit = jnp.left_shift(jnp.int32(1), jnp.right_shift(ids, 7))
        word = jnp.zeros((STEP, STEP), jnp.int32)
        for j in range(LISTED):
            word = word | jnp.where(low[:, j:j + 1] == lane, bit[:, j:j + 1], 0)
        tail = down(tail_ref[:, at])
        keep = jnp.where((tail & 127) == lane, jnp.left_shift(jnp.int32(1), jnp.right_shift(tail, 7)), 0)
        word_ref[at] = (word & ~keep) | jnp.left_shift(keep, 8)
        return 0

    spread.take_z(0)
    spread.take_b(0)
    lax.fori_loop(0, 1, prepare, 0)
    spread.take_z(1)
    spread.take_z(2)
    lax.fori_loop(1, 2, prepare, 0)
    for q in (1, 2, 3):
        spread.take_b(q)
    for j in range(4):
        push(j, ga, (gb + j) % 4)
    lax.fori_loop(2, 4, prepare, 0)
    for j in (0, 3, 1, 2):
        for q in range(4):
            spread.take_a(q, j)
        for k in (1, 3, 2):
            push(4 * k + j, (ga + 4 - k) % 4, (gb + j) % 4)
    for i in range(16):
        w.wait(tp[i], table_ref.at[other, pl.ds(0, 64)], partner)

    def squares(i, _):
        re, im = table_ref[0, span(i, STEP)].astype(F32), table_ref[1, span(i, STEP)].astype(F32)
        s = jnp.sum(re * re + im * im, axis=1, keepdims=True)
        square_ref[i] = jnp.transpose(jnp.broadcast_to(s, (STEP, STEP)))[0:8]
        return 0

    lax.fori_loop(0, 8, squares, 0)

    def main(i, _):
        at = span(i, MAIN)
        hot = hot_rows(head_ref[at])
        c, s = cos_ref[at], sin_ref[at]
        hr, hm = dot(hot, table_ref[0]), dot(hot, table_ref[1])
        qr = hr * c - hm * s
        qm = hr * s + hm * c
        query_r, query_m = qr.astype(BF16), qm.astype(BF16)
        query_ref[0, at] = query_r
        query_ref[1, at] = query_m
        near_r, near_m = query_r.astype(F32), query_m.astype(F32)
        query_sq = jnp.sum(near_r * near_r + near_m * near_m, axis=1, keepdims=True)
        cross = dot_nt(query_r, table_ref[0]) + dot_nt(query_m, table_ref[1])
        word = word_ref[at]
        scores, hidden = [], []
        top = None
        for k in range(8):
            sc = 2.0 * cross[:, k * 128:(k + 1) * 128] - query_sq - square_ref[k, 0:1]
            hide = (word & (1 << k)) != 0
            scores.append(sc)
            hidden.append(hide)
            seen = jnp.where(hide, -jnp.inf, sc)
            top = seen if top is None else jnp.maximum(top, seen)
        top = jnp.max(top, axis=1, keepdims=True)
        raws = []
        for k in range(8):
            raws.append(jnp.where(hidden[k], 0.0, jnp.exp(scores[k] - top)))
        total = raws[0]
        for k in range(1, 8):
            total = total + raws[k]
        scale = 2.0 / jnp.sum(total, axis=1, keepdims=True)
        weights = []
        for k in range(8):
            hit = (word & (256 << k)) != 0
            wk = (raws[k] * scale - jnp.where(hit, 2.0, 0.0)).astype(BF16)
            weights.append(wk)
            weight_ref[k, at] = wk
        both = jnp.concatenate(weights, axis=1)
        gr, gm = dot(both, table_ref[0]), dot(both, table_ref[1])
        back_ref[0, at] = (gr * c + gm * s).astype(BF16)
        back_ref[1, at] = (gm * c - gr * s).astype(BF16)
        turn = qr * gm - qm * gr
        high = turn.astype(BF16)
        turn_ref[0, at] = high
        turn_ref[1, at] = (turn - high.astype(F32)).astype(BF16)
        return 0

    lax.fori_loop(0, TRIPLES // MAIN, main, 0)

    def key(i):
        return lax.broadcasted_iota(jnp.int32, (DENSE, 1), 0) + i * DENSE

    def relations(i, _):
        hot = (relation_ref[...] == key(i)).astype(F32).astype(BF16)
        d_ref[span(i, DENSE)] = dot(hot, turn_ref[0]) + dot(hot, turn_ref[1])
        return 0

    lax.fori_loop(0, 1024 // DENSE, relations, 0)

    def d_load(a, b, k):
        px, py = dxy(a, b)
        return d_ref[span((px * 4 + py) * 4 + k, 16)]

    d_chain = Chain(w, d_load, dto, da, db, zh, (da_out, da_in, d_small, db_out, db_in, d_sum))
    for q in range(4):
        d_chain.begin_a(q)

    ones = jnp.ones((TRIPLES, 128), BF16)
    heads = owner_ref[...] * 4 + place_ref[...]

    def dense(i):
        at = span(i, DENSE)
        wk = jnp.concatenate([weight_ref[i * (DENSE // 128) + k] for k in range(DENSE // 128)], axis=1)
        counts = dot_tn(wk, ones)
        hot = (heads == key(i)).astype(F32).astype(BF16)
        many = jnp.concatenate([counts] * 4, axis=1)
        for c in range(2):
            sums = dot_tn(wk, query_ref[c]) + dot(hot, back_ref[c])
            g_ref[c, at] = sums - many * table_ref[c, at].astype(F32)

    tg = [w.number() for _ in range(4)]

    def dense_of(n):
        i = (x + 2 + n) % 4
        dense(i)
        w.start(tg[n], g_ref.at[other, span(i, DENSE)], pair.at[span(i, DENSE)], partner)

    dense_of(0)
    dense_of(1)
    d_chain.turn_b(0)
    dense_of(2)
    d_chain.turn_b(1)
    dense_of(3)
    d_chain.turn_b(2)
    d_chain.turn_b(3)
    for n in range(4):
        w.wait(tg[n], pair.at[span((x + 2 + n) % 4, DENSE)], partner)

    def g_load(a, b, k):
        px, py = gxy(a, b)
        at = span((px * 4 + py) * 4 + k, 16)
        return g_ref[core, at] + pair[at]

    g_chain = Chain(w, g_load, gto, ga, gb, zh, (ga_out, ga_in, g_small, gb_out, gb_in, g_sum))
    for q in range(4):
        g_chain.begin_a(q)

    tdz = [w.number() for _ in range(3)]
    for q in range(4):
        d_chain.end_b(q)
        if FAR[q]:
            to = device(x, y, (zh + FAR[q]) % 4, zl, core)
            w.start(tdz[FAR[q] - 1], d_sum.at[q], d_zin.at[FAR[q] - 1], to)
    g_chain.turn_b(0)
    for k in (1, 3, 2):
        w.wait(tdz[k - 1], d_zin.at[k - 1], partner)

    def r_block(a, b, k):
        px, py = dxy(a, b)
        return r_ref.at[span((px * 4 + py) * 4 + k, 16)]

    r_block(da, db, zh)[...] = (d_sum[3] + ((d_zin[0] + d_zin[2]) + d_zin[1])).astype(r_ref.dtype)
    back = Spread(w, r_block, dto, da, db, zh, [device(x, y, (zh + k) % 4, zl, core) for k in (1, 3, 2)],
                  [(zh + 4 - k) % 4 for k in (1, 3, 2)])
    back.begin()

    tgz = [[w.number() for _ in range(2)] for _ in range(4)]
    here = [(FAR.index(off), off, dl) for off in FAR for dl in range(2)]
    here = [(q, off, dl) for q, off, dl in here if off or dl]

    def end_g(q):
        g_chain.end_b(q)
        for qq, off, dl in here:
            if qq == q:
                ll = (zl + dl) % 2
                w.start(tgz[off][dl], g_sum.at[q, span(ll, 8)], g_zin.at[off, dl], device(x, y, (zh + off) % 4, ll, core))

    g_chain.turn_b(1)
    g_chain.turn_b(2)
    g_chain.turn_b(3)
    back.take_z(0)
    back.take_b(0)
    end_g(0)
    end_g(1)
    back.take_z(1)
    back.take_z(2)
    end_g(2)
    end_g(3)
    back.take_b(1)
    back.take_b(2)
    back.take_b(3)
    total = g_sum[3, span(zl, 8)]
    for q, off, dl in here:
        w.wait(tgz[off][dl], g_zin.at[off, dl], partner)
        total = total + g_zin[off, dl]
    g_last[...] = total
    ts = w.number()
    w.start(ts, g_last, g_swap, partner)
    for q in range(4):
        back.take_a(q, 0)
    w.wait(ts, g_swap, partner)
    first, second = g_last[...], g_swap[...]
    left = jnp.where(core == 0, first, second)
    right = jnp.where(core == 0, second, first)
    e_ref[:, 0:COLS] = jnp.where(core == 0, left[0:4], left[4:8])
    e_ref[:, COLS:2 * COLS] = jnp.where(core == 0, right[0:4], right[4:8])
    for j in (3, 1, 2):
        for q in range(4):
            back.take_a(q, j)
    w.drain()


def local(entity_table, phases, head_owner, head_row, relation, tail_ids, known_tails):
    messages = 16 + 63 + 24 + 4 + 24 + 3 + 63 + 8 + 1
    here = pl.BlockSpec(memory_space=VMEM)
    e, r = pl.pallas_call(
        step_kernel,
        out_shape=(jax.ShapeDtypeStruct((4, 2 * COLS), F32), jax.ShapeDtypeStruct((1024, COLS), WIRE)),
        in_specs=[here] * 5 + [pl.BlockSpec(memory_space=pltpu.HBM), here],
        out_specs=[here, here],
        scratch_shapes=[
            pltpu.SemaphoreType.DMA((messages,)),
            pltpu.SemaphoreType.DMA((messages,)),
            pltpu.SemaphoreType.DMA,
            pltpu.SemaphoreType.DMA,
            VMEM((1024, COLS), F32),
            VMEM((3, 1024, COLS), BF16),
            VMEM((TRIPLES, COLS), F32),
            VMEM((TRIPLES, COLS), F32),
            VMEM((TRIPLES, STEP), jnp.int32),
            VMEM((TRIPLES, STEP), jnp.int32),
            VMEM((2, 1024, COLS), BF16),
            VMEM((8, 8, STEP), F32),
            VMEM((2, TRIPLES, COLS), BF16),
            VMEM((8, TRIPLES, STEP), BF16),
            VMEM((2, TRIPLES, COLS), BF16),
            VMEM((2, TRIPLES, COLS), BF16),
            VMEM((2, 1024, COLS), F32),
            VMEM((1024, COLS), F32),
            VMEM((1024, COLS), F32),
            VMEM((3, 4, 4, 16, COLS), WIRE),
            VMEM((3, 4, 4, 16, COLS), WIRE),
            VMEM((4, 4, 16, COLS), F32),
            VMEM((3, 4, 16, COLS), WIRE),
            VMEM((3, 4, 16, COLS), WIRE),
            VMEM((4, 16, COLS), F32),
            VMEM((4, 2, 8, COLS), F32),
            VMEM((8, COLS), F32),
            VMEM((8, COLS), F32),
            VMEM((3, 4, 4, 16, COLS), WIRE),
            VMEM((3, 4, 4, 16, COLS), WIRE),
            VMEM((4, 4, 16, COLS), F32),
            VMEM((3, 4, 16, COLS), WIRE),
            VMEM((3, 4, 16, COLS), WIRE),
            VMEM((4, 16, COLS), F32),
            VMEM((3, 16, COLS), F32),
        ],
        compiler_params=pltpu.CompilerParams(collective_id=0, has_side_effects=True, vmem_limit_bytes=36 << 20),
        name="step",
    )(known_tails.T, head_owner.reshape(1, TRIPLES), head_row.reshape(1, TRIPLES), relation.reshape(1, TRIPLES),
      tail_ids.reshape(1, TRIPLES), phases, entity_table)
    return e, r.astype(F32)


def solution(mesh):
    in_specs = (
        P("ent", None),
        P("rel", None),
        P(("ent", "rel"), None),
        P(("ent", "rel")),
        P(("ent", "rel")),
        P(("ent", "rel")),
        P(("ent", "rel"), None),
    )
    out_specs = (P(("ent", "rel"), None), P("rel", None))
    return jax.shard_map(local, mesh=mesh, in_specs=in_specs, out_specs=out_specs, check_vma=False)
```

time: 84.4 us -> 75.9 us (0.90)
  the two profiles are of different devices: /device:TPU:8 before, /device:TPU:1 now
where the time goes in v3:
time: 75.9 us; the launch traced here: 75.6 us
  Pallas kernels  66.8 us (88%)
  local copies, waits for them, and re-layouts  6.51 us (9%)
  other arithmetic  1.61 us (2%)
    pallas_call x1, Pallas kernels, local(): pl.pallas_call(step_kernel, out_shape=(jax.ShapeDtypeStruct((4, 2 * COLS)...  66.8 us
    unnamed x15, local copies, waits for them, and re-layouts  6.51 us
    convert_element_type x1, other arithmetic, local(): return (e, r.astype(F32))  1.61 us

profile of v3, /device:TPU:1, one launch (start us, length us, event | category | flops | bytes accessed | tf_op | source)
XLA Modules:
  0.0 75.6 jit_solution(17274488923412786778)
XLA Ops:
  0.6 0.0 copy-start
  0.6 1.6 %copy-done = f32[1024,512]{1,0:T(8,128)S(1)} copy-done((f32[1024,512]{1,0:T(8,128)S(1)}, f32[1024,512]{1,0:T(8,128)}, u32[]{:S(2)}) %copy-start) | copy-done | bytes 2097176
  2.2 0.0 copy-start.1
  2.2 0.8 %copy-done.1 = s32[512,32]{0,1:T(8,128)S(1)} copy-done((s32[512,32]{0,1:T(8,128)S(1)}, s32[512,32]{0,1:T(8,128)}, u32[]{:S(2)}) %copy-start.1) | copy-done | bytes 65560
  3.1 0.0 copy-start.2
  3.1 0.8 copy-done.2
  3.8 0.0 copy-start.3
  3.8 0.7 copy-done.3
  4.5 0.0 copy-start.4
  4.5 0.7 copy-done.4
  5.2 0.0 copy-start.5
  5.2 0.7 copy-done.5
  5.9 0.0 copy-start.6
  5.9 0.7 copy-done.6
  6.6 66.8 %step.1 = (f32[4,1024]{1,0:T(4,128)S(1)}, bf16[1024,512]{1,0:T(8,128)(2,1)S(1)}) custom-call(s32[32,512]{1,0:T(8,128)S(1)} %bitcast.5, s32[1,512]{1,0:T(1,128)S(1)} %bitcast.6, s32[1,512]{1,0:T(1,128)S(1)} %bitcast.7, s32[1,512]{1,0:T(1,128)S(1)} %bitcast.8, s32[1,512]{1,0:T(1,128)S(1)} %bitcast.9, f32[1024,512]{1,0:T(8,128)S(1)} %copy-done, ...), custom_call_target="tpu_custom_call" | custom-call | tf_op jit(solution)/shard_map/step/pallas_call | solution.py:490
  73.4 1.6 %convert_element_type.3 = f32[1024,512]{1,0:T(8,128)} convert(bf16[1024,512]{1,0:T(8,128)(2,1)S(1)} %get-tuple-element.5) | non-fusion elementwise | flops 524288 | bytes 3145728 | tf_op jit(solution)/shard_map/convert_element_type | solution.py:536
  75.0 0.6 copy.10
Async XLA Ops:
  0.6 1.6 %copy-start = (f32[1024,512]{1,0:T(8,128)S(1)}, f32[1024,512]{1,0:T(8,128)}, u32[]{:S(2)}) copy-start(f32[1024,512]{1,0:T(8,128)} %phases_hbm.1) | copy-start | bytes 6291460
  2.2 0.8 %copy-start.1 = (s32[512,32]{0,1:T(8,128)S(1)}, s32[512,32]{0,1:T(8,128)}, u32[]{:S(2)}) copy-start(s32[512,32]{0,1:T(8,128)} %param.13) | copy-start | bytes 196612
  3.1 0.8 %copy-start.2 = (bf16[16,1024]{1,0:T(8,128)(2,1)S(1)}, bf16[16,1024]{1,0:T(8,128)(2,1)}, u32[]{:S(2)}) copy-start(bf16[16,1024]{1,0:T(8,128)(2,1)} %entity_ref.1) | copy-start | bytes 98308
  3.8 0.7 copy-start.3
  4.5 0.7 copy-start.4
  5.2 0.7 copy-start.5
  5.9 0.7 copy-start.6

commit v4 on v3

--- a/solution.py
+++ b/solution.py
@@ -78,14 +78,14 @@
         peers.append(device(x, y, zz // 2, zz % 2, core))
     for peer in peers:
         pl.semaphore_signal(barrier, inc=1, device_id=peer, device_id_type=MESH)
-    pl.semaphore_wait(barrier, len(peers))
+    return lambda: pl.semaphore_wait(barrier, len(peers))
 
 
 class Spread:
-    def __init__(self, wire, block, to, a0, b0, own, z_to, z_from):
+    def __init__(self, wire, block, to, a0, b0, ks, z_to):
         self.w, self.block, self.to, self.a0, self.b0 = wire, block, to, a0, b0
-        self.z_to, self.ks = z_to, [own] + z_from
-        self.tz = [wire.number() for _ in range(3)]
+        self.z_to, self.ks = z_to, ks
+        self.tz = [wire.number() for _ in z_to]
         self.tb = [[wire.number() for _ in range(3)] for _ in range(4)]
         self.ta = [[[wire.number() for _ in range(3)] for _ in range(4)] for _ in range(4)]
 
@@ -127,9 +127,9 @@
 
 
 class Chain:
-    def __init__(self, wire, load, to, a0, b0, zh, bufs):
+    def __init__(self, wire, load, to, a0, b0, ks, bufs):
         self.w, self.load, self.to, self.a0, self.b0 = wire, load, to, a0, b0
-        self.ks = [(zh + off) % 4 for off in FAR]
+        self.ks = ks
         self.out_a, self.in_a, self.small, self.out_b, self.in_b, self.last = bufs
         self.ta = [[wire.number() for _ in range(3)] for _ in range(4)]
         self.tb = [[wire.number() for _ in range(3)] for _ in range(4)]
@@ -177,15 +177,15 @@
 
 
 STEP = 128
-MAIN = 256
+MAIN = 512
 DENSE = 256
 TRIPLES = 512
 LISTED = 32
 
 
-def step_kernel(known_ref, owner_ref, place_ref, relation_ref, tail_ref, phases_hbm, entity_ref, e_ref, r_ref,
-                send, recv, local_sem, phases_sem,
-                phases_ref, parts, cos_ref, sin_ref, word_ref, head_ref, table_ref, square_ref,
+def step_kernel(known_hbm, owner_hbm, place_hbm, relation_hbm, tail_hbm, phases_hbm, entity_hbm, e_ref, r_ref,
+                send, recv, local_sem,
+                known_ref, owner_ref, place_ref, relation_ref, tail_ref, phases_ref, parts, cos_ref, sin_ref, word_ref, head_ref, table_ref, square_ref,
                 query_ref, weight_ref, back_ref, turn_ref, g_ref, pair, d_ref,
                 ga_out, ga_in, g_small, gb_out, gb_in, g_sum, g_zin, g_last, g_swap,
                 da_out, da_in, d_small, db_out, db_in, d_sum, d_zin):
@@ -197,8 +197,6 @@
     partner = device(x, y, zh, zl, other)
     w = Wire(send, recv)
 
-    fetch = pltpu.make_async_copy(phases_hbm, phases_ref, phases_sem)
-    fetch.start()
     ga, gb = x * other + y * core, y * other + x * core
     da, db = gb, ga
 
@@ -224,7 +222,7 @@
         px, py = dxy(a, b)
         return device(px, py, zh, zl, core)
 
-    greet(x, y, zh, zl, core)
+    everyone = greet(x, y, zh, zl, core)
 
     tp = [w.number() for _ in range(16)]
 
@@ -235,17 +233,24 @@
     z_to = [device(x, y, (zh + z_sign + 4) % 4, 1 - zl, core), device(x, y, (zh + z_sign + 4) % 4, zl, core),
             device(x, y, (zh + 2) % 4, 1 - zl, core)]
     z_from = [(zh + z_sign + 4) % 4, (zh - z_sign + 4) % 4, (zh + 2) % 4]
-    own = pltpu.make_async_copy(entity_ref.at[:, mine], block(ga, gb, zh), local_sem)
+    own = pltpu.make_async_copy(entity_hbm.at[:, mine], block(ga, gb, zh), local_sem.at[0])
     own.start()
+    pairs = ((phases_hbm, phases_ref), (known_hbm, known_ref), (owner_hbm, owner_ref), (place_hbm, place_ref),
+             (relation_hbm, relation_ref), (tail_hbm, tail_ref))
+    fetches = [pltpu.make_async_copy(a, b, local_sem.at[1 + i]) for i, (a, b) in enumerate(pairs)]
+    for f in fetches:
+        f.start()
     own.wait()
-    spread = Spread(w, block, gto, ga, gb, zh, z_to, z_from)
+    everyone()
+    spread = Spread(w, block, gto, ga, gb, [zh] + z_from, z_to)
     spread.begin()
 
     def push(i, a, b):
         part = table_ref.at[core, gspan(a, b)]
         w.start(tp[i], part, part, partner)
 
-    fetch.wait()
+    for f in fetches:
+        f.wait()
 
     def split(i, _):
         at = span(i, STEP)
@@ -375,7 +380,7 @@
         px, py = dxy(a, b)
         return d_ref[span((px * 4 + py) * 4 + k, 16)]
 
-    d_chain = Chain(w, d_load, dto, da, db, zh, (da_out, da_in, d_small, db_out, db_in, d_sum))
+    d_chain = Chain(w, d_load, dto, da, db, list(range(4)), (da_out, da_in, d_small, db_out, db_in, d_sum))
     for q in range(4):
         d_chain.begin_a(q)
 
@@ -399,44 +404,55 @@
         dense(i)
         w.start(tg[n], g_ref.at[other, span(i, DENSE)], pair.at[span(i, DENSE)], partner)
 
+    tdz = [[w.number() for _ in range(3)] for _ in range(4)]
+
+    def share(q):
+        d_chain.end_b(q)
+        d_zin[zh, q] = d_sum[q].astype(d_zin.dtype)
+        for k in (2, 1, 3):
+            to = device(x, y, (zh + k) % 4, zl, core)
+            w.start(tdz[q][k - 1], d_zin.at[zh, q], d_zin.at[zh, q], to)
+
+    def r_block(a, b, k):
+        px, py = dxy(a, b)
+        return r_ref.at[span((px * 4 + py) * 4 + k, 16)]
+
+    back = Spread(w, r_block, dto, da, db, list(range(4)), [])
+
+    def settle(q):
+        for k in (1, 3, 2):
+            w.wait(tdz[q][k - 1], d_zin.at[(zh + 4 - k) % 4, q], partner)
+        z = [d_zin[k, q].astype(F32) for k in range(4)]
+        r_block(da, db, q)[...] = ((z[0] + z[1]) + (z[2] + z[3])).astype(r_ref.dtype)
+        back.on(q)
+
     dense_of(0)
     dense_of(1)
     d_chain.turn_b(0)
     dense_of(2)
     d_chain.turn_b(1)
+    share(0)
     dense_of(3)
     d_chain.turn_b(2)
+    share(1)
     d_chain.turn_b(3)
-    for n in range(4):
-        w.wait(tg[n], pair.at[span((x + 2 + n) % 4, DENSE)], partner)
+    share(2)
 
     def g_load(a, b, k):
         px, py = gxy(a, b)
         at = span((px * 4 + py) * 4 + k, 16)
         return g_ref[core, at] + pair[at]
 
-    g_chain = Chain(w, g_load, gto, ga, gb, zh, (ga_out, ga_in, g_small, gb_out, gb_in, g_sum))
-    for q in range(4):
-        g_chain.begin_a(q)
-
-    tdz = [w.number() for _ in range(3)]
-    for q in range(4):
-        d_chain.end_b(q)
-        if FAR[q]:
-            to = device(x, y, (zh + FAR[q]) % 4, zl, core)
-            w.start(tdz[FAR[q] - 1], d_sum.at[q], d_zin.at[FAR[q] - 1], to)
-    g_chain.turn_b(0)
-    for k in (1, 3, 2):
-        w.wait(tdz[k - 1], d_zin.at[k - 1], partner)
-
-    def r_block(a, b, k):
-        px, py = dxy(a, b)
-        return r_ref.at[span((px * 4 + py) * 4 + k, 16)]
-
-    r_block(da, db, zh)[...] = (d_sum[3] + ((d_zin[0] + d_zin[2]) + d_zin[1])).astype(r_ref.dtype)
-    back = Spread(w, r_block, dto, da, db, zh, [device(x, y, (zh + k) % 4, zl, core) for k in (1, 3, 2)],
-                  [(zh + 4 - k) % 4 for k in (1, 3, 2)])
-    back.begin()
+    g_chain = Chain(w, g_load, gto, ga, gb, [(zh + off) % 4 for off in FAR],
+                    (ga_out, ga_in, g_small, gb_out, gb_in, g_sum))
+    for n in range(4):
+        w.wait(tg[n], pair.at[span((x + 2 + n) % 4, DENSE)], partner)
+    g_chain.begin_a(0)
+    g_chain.begin_a(1)
+    share(3)
+    settle(0)
+    g_chain.begin_a(2)
+    g_chain.begin_a(3)
 
     tgz = [[w.number() for _ in range(2)] for _ in range(4)]
     here = [(FAR.index(off), off, dl) for off in FAR for dl in range(2)]
@@ -449,20 +465,21 @@
                 ll = (zl + dl) % 2
                 w.start(tgz[off][dl], g_sum.at[q, span(ll, 8)], g_zin.at[off, dl], device(x, y, (zh + off) % 4, ll, core))
 
+    settle(1)
+    settle(2)
+    g_chain.turn_b(0)
+    settle(3)
+    back.take_b(0)
     g_chain.turn_b(1)
+    back.take_b(1)
     g_chain.turn_b(2)
+    back.take_b(2)
     g_chain.turn_b(3)
-    back.take_z(0)
-    back.take_b(0)
     end_g(0)
+    back.take_b(3)
     end_g(1)
-    back.take_z(1)
-    back.take_z(2)
     end_g(2)
     end_g(3)
-    back.take_b(1)
-    back.take_b(2)
-    back.take_b(3)
     total = g_sum[3, span(zl, 8)]
     for q, off, dl in here:
         w.wait(tgz[off][dl], g_zin.at[off, dl], partner)
@@ -485,18 +502,22 @@
 
 
 def local(entity_table, phases, head_owner, head_row, relation, tail_ids, known_tails):
-    messages = 16 + 63 + 24 + 4 + 24 + 3 + 63 + 8 + 1
+    messages = 16 + 63 + 24 + 4 + 24 + 12 + 60 + 8 + 1
     here = pl.BlockSpec(memory_space=VMEM)
     e, r = pl.pallas_call(
         step_kernel,
         out_shape=(jax.ShapeDtypeStruct((4, 2 * COLS), F32), jax.ShapeDtypeStruct((1024, COLS), WIRE)),
-        in_specs=[here] * 5 + [pl.BlockSpec(memory_space=pltpu.HBM), here],
+        in_specs=[pl.BlockSpec(memory_space=pltpu.HBM)] * 7,
         out_specs=[here, here],
         scratch_shapes=[
             pltpu.SemaphoreType.DMA((messages,)),
             pltpu.SemaphoreType.DMA((messages,)),
-            pltpu.SemaphoreType.DMA,
-            pltpu.SemaphoreType.DMA,
+            pltpu.SemaphoreType.DMA((7,)),
+            VMEM((LISTED, TRIPLES), jnp.int32),
+            VMEM((1, TRIPLES), jnp.int32),
+            VMEM((1, TRIPLES), jnp.int32),
+            VMEM((1, TRIPLES), jnp.int32),
+            VMEM((1, TRIPLES), jnp.int32),
             VMEM((1024, COLS), F32),
             VMEM((3, 1024, COLS), BF16),
             VMEM((TRIPLES, COLS), F32),
@@ -527,12 +548,13 @@
             VMEM((3, 4, 16, COLS), WIRE),
             VMEM((3, 4, 16, COLS), WIRE),
             VMEM((4, 16, COLS), F32),
-            VMEM((3, 16, COLS), F32),
+            VMEM((4, 4, 16, COLS), WIRE),
         ],
         compiler_params=pltpu.CompilerParams(collective_id=0, has_side_effects=True, vmem_limit_bytes=36 << 20),
         name="step",
-    )(known_tails.T, head_owner.reshape(1, TRIPLES), head_row.reshape(1, TRIPLES), relation.reshape(1, TRIPLES),
-      tail_ids.reshape(1, TRIPLES), phases, entity_table)
+    )(*(pltpu.with_memory_space_constraint(v, pltpu.HBM) for v in (
+        known_tails.T, head_owner.reshape(1, TRIPLES), head_row.reshape(1, TRIPLES), relation.reshape(1, TRIPLES),
+        tail_ids.reshape(1, TRIPLES), phases, entity_table)))
     return e, r.astype(F32)
 
 

time: 75.9 us -> 75.7 us (level)
  Pallas kernels: 66.8 us -> 72.8 us
  local copies, waits for them, and re-layouts: 6.51 us -> 0.6 us
    pallas_call x1, Pallas kernels: 66.8 us -> 72.8 us  [local(): pl.pallas_call(step_kernel, out_shape=(jax.ShapeDtypeStruct((4, 2 * COLS)...]
    unnamed x15 -> x1, local copies, waits for them, and re-layouts: 6.51 us -> 0.6 us
where the time goes in v4:
time: 75.7 us; the launch traced here: 75.6 us
  Pallas kernels  72.8 us (96%)
  other arithmetic  1.61 us (2%)
    pallas_call x1, Pallas kernels, local(): pl.pallas_call(step_kernel, out_shape=(jax.ShapeDtypeStruct((4, 2 * COLS)...  72.8 us
    convert_element_type x1, other arithmetic, local(): return (e, r.astype(F32))  1.61 us

profile of v4, /device:TPU:1, one launch (start us, length us, event | category | flops | bytes accessed | tf_op | source)
XLA Modules:
  0.0 75.6 jit_solution(7413793362101243419)
XLA Ops:
  0.6 72.8 %step.1 = (f32[4,1024]{1,0:T(4,128)S(1)}, bf16[1024,512]{1,0:T(8,128)(2,1)S(1)}) custom-call(s32[32,512]{1,0:T(8,128)} %bitcast.5, s32[1,512]{1,0:T(1,128)} %bitcast.6, s32[1,512]{1,0:T(1,128)} %bitcast.7, s32[1,512]{1,0:T(1,128)} %bitcast.8, s32[1,512]{1,0:T(1,128)} %bitcast.9, f32[1024,512]{1,0:T(8,128)} %phases_hbm.1, bf16[16,1024]{1,0:T(8,128)(2,1)} %entity_hbm.1), custom_call_target="tpu_custom_call" | custom-call | tf_op jit(solution)/shard_map/step/pallas_call | solution.py:507
  73.4 1.6 %convert_element_type.3 = f32[1024,512]{1,0:T(8,128)} convert(bf16[1024,512]{1,0:T(8,128)(2,1)S(1)} %get-tuple-element.5) | non-fusion elementwise | flops 524288 | bytes 3145728 | tf_op jit(solution)/shard_map/convert_element_type | solution.py:558
  75.0 0.6 copy.10

commit v5 on v4

--- a/solution.py
+++ b/solution.py
@@ -426,18 +426,6 @@
         r_block(da, db, q)[...] = ((z[0] + z[1]) + (z[2] + z[3])).astype(r_ref.dtype)
         back.on(q)
 
-    dense_of(0)
-    dense_of(1)
-    d_chain.turn_b(0)
-    dense_of(2)
-    d_chain.turn_b(1)
-    share(0)
-    dense_of(3)
-    d_chain.turn_b(2)
-    share(1)
-    d_chain.turn_b(3)
-    share(2)
-
     def g_load(a, b, k):
         px, py = gxy(a, b)
         at = span((px * 4 + py) * 4 + k, 16)
@@ -445,15 +433,6 @@
 
     g_chain = Chain(w, g_load, gto, ga, gb, [(zh + off) % 4 for off in FAR],
                     (ga_out, ga_in, g_small, gb_out, gb_in, g_sum))
-    for n in range(4):
-        w.wait(tg[n], pair.at[span((x + 2 + n) % 4, DENSE)], partner)
-    g_chain.begin_a(0)
-    g_chain.begin_a(1)
-    share(3)
-    settle(0)
-    g_chain.begin_a(2)
-    g_chain.begin_a(3)
-
     tgz = [[w.number() for _ in range(2)] for _ in range(4)]
     here = [(FAR.index(off), off, dl) for off in FAR for dl in range(2)]
     here = [(q, off, dl) for q, off, dl in here if off or dl]
@@ -465,39 +444,71 @@
                 ll = (zl + dl) % 2
                 w.start(tgz[off][dl], g_sum.at[q, span(ll, 8)], g_zin.at[off, dl], device(x, y, (zh + off) % 4, ll, core))
 
+    ts = w.number()
+
+    def pairs_in():
+        for n in range(4):
+            w.wait(tg[n], pair.at[span((x + 2 + n) % 4, DENSE)], partner)
+
+    def send_last():
+        total = g_sum[3, span(zl, 8)]
+        for q, off, dl in here:
+            w.wait(tgz[off][dl], g_zin.at[off, dl], partner)
+            total = total + g_zin[off, dl]
+        g_last[...] = total
+        w.start(ts, g_last, g_swap, partner)
+
+    def finish():
+        w.wait(ts, g_swap, partner)
+        first, second = g_last[...], g_swap[...]
+        left = jnp.where(core == 0, first, second)
+        right = jnp.where(core == 0, second, first)
+        e_ref[:, 0:COLS] = jnp.where(core == 0, left[0:4], left[4:8])
+        e_ref[:, COLS:2 * COLS] = jnp.where(core == 0, right[0:4], right[4:8])
+
+    def ahead(j):
+        for q in range(4):
+            back.take_a(q, j)
+
+    dense_of(0)
+    dense_of(1)
+    dense_of(2)
+    dense_of(3)
+    d_chain.turn_b(0)
+    d_chain.turn_b(1)
+    pairs_in()
+    g_chain.begin_a(0)
+    g_chain.begin_a(1)
+    d_chain.turn_b(2)
+    d_chain.turn_b(3)
+    g_chain.begin_a(2)
+    g_chain.begin_a(3)
+    share(0)
+    share(1)
+    share(2)
+    share(3)
+    g_chain.turn_b(0)
+    g_chain.turn_b(1)
+    g_chain.turn_b(2)
+    g_chain.turn_b(3)
+    settle(0)
     settle(1)
     settle(2)
-    g_chain.turn_b(0)
     settle(3)
     back.take_b(0)
-    g_chain.turn_b(1)
+    end_g(0)
     back.take_b(1)
-    g_chain.turn_b(2)
+    end_g(1)
     back.take_b(2)
-    g_chain.turn_b(3)
-    end_g(0)
+    end_g(2)
     back.take_b(3)
-    end_g(1)
-    end_g(2)
     end_g(3)
-    total = g_sum[3, span(zl, 8)]
-    for q, off, dl in here:
-        w.wait(tgz[off][dl], g_zin.at[off, dl], partner)
-        total = total + g_zin[off, dl]
-    g_last[...] = total
-    ts = w.number()
-    w.start(ts, g_last, g_swap, partner)
-    for q in range(4):
-        back.take_a(q, 0)
-    w.wait(ts, g_swap, partner)
-    first, second = g_last[...], g_swap[...]
-    left = jnp.where(core == 0, first, second)
-    right = jnp.where(core == 0, second, first)
-    e_ref[:, 0:COLS] = jnp.where(core == 0, left[0:4], left[4:8])
-    e_ref[:, COLS:2 * COLS] = jnp.where(core == 0, right[0:4], right[4:8])
-    for j in (3, 1, 2):
-        for q in range(4):
-            back.take_a(q, j)
+    send_last()
+    finish()
+    ahead(0)
+    ahead(3)
+    ahead(1)
+    ahead(2)
     w.drain()
 
 

time: 75.7 us -> 68.2 us (0.901)
  Pallas kernels: 72.8 us -> 65.2 us
    pallas_call x1, Pallas kernels: 72.8 us -> 65.2 us  [local(): pl.pallas_call(step_kernel, out_shape=(jax.ShapeDtypeStruct((4, 2 * COLS)...]
where the time goes in v5:
time: 68.2 us; the launch traced here: 68.1 us
  Pallas kernels  65.2 us (96%)
  other arithmetic  1.61 us (2%)
    pallas_call x1, Pallas kernels, local(): pl.pallas_call(step_kernel, out_shape=(jax.ShapeDtypeStruct((4, 2 * COLS)...  65.2 us
    convert_element_type x1, other arithmetic, local(): return (e, r.astype(F32))  1.61 us

profile of v5, /device:TPU:1, one launch (start us, length us, event | category | flops | bytes accessed | tf_op | source)
XLA Modules:
  0.0 68.1 jit_solution(16315663249972274724)
XLA Ops:
  0.6 65.2 %step.1 = (f32[4,1024]{1,0:T(4,128)S(1)}, bf16[1024,512]{1,0:T(8,128)(2,1)S(1)}) custom-call(s32[32,512]{1,0:T(8,128)} %bitcast.5, s32[1,512]{1,0:T(1,128)} %bitcast.6, s32[1,512]{1,0:T(1,128)} %bitcast.7, s32[1,512]{1,0:T(1,128)} %bitcast.8, s32[1,512]{1,0:T(1,128)} %bitcast.9, f32[1024,512]{1,0:T(8,128)} %phases_hbm.1, bf16[16,1024]{1,0:T(8,128)(2,1)} %entity_hbm.1), custom_call_target="tpu_custom_call" | custom-call | tf_op jit(solution)/shard_map/step/pallas_call | solution.py:518
  65.9 1.6 %convert_element_type.3 = f32[1024,512]{1,0:T(8,128)} convert(bf16[1024,512]{1,0:T(8,128)(2,1)S(1)} %get-tuple-element.5) | non-fusion elementwise | flops 524288 | bytes 3145728 | tf_op jit(solution)/shard_map/convert_element_type | solution.py:569
  67.5 0.6 copy.10

commit v6 on v5

--- a/solution.py
+++ b/solution.py
@@ -185,7 +185,7 @@
 
 def step_kernel(known_hbm, owner_hbm, place_hbm, relation_hbm, tail_hbm, phases_hbm, entity_hbm, e_ref, r_ref,
                 send, recv, local_sem,
-                known_ref, owner_ref, place_ref, relation_ref, tail_ref, phases_ref, parts, cos_ref, sin_ref, word_ref, head_ref, table_ref, square_ref,
+                known_ref, owner_ref, place_ref, relation_ref, tail_ref, phases_ref, parts, cos_ref, sin_ref, word_ref, hot_ref, head_ref, table_ref, square_ref,
                 query_ref, weight_ref, back_ref, turn_ref, g_ref, pair, d_ref,
                 ga_out, ga_in, g_small, gb_out, gb_in, g_sum, g_zin, g_last, g_swap,
                 da_out, da_in, d_small, db_out, db_in, d_sum, d_zin):
@@ -273,7 +273,7 @@
 
     def prepare(i, _):
         at = span(i, STEP)
-        head_ref[at] = down(owner_ref[:, at] * 4 + place_ref[:, at])
+        hot_ref[at] = hot_rows(down(owner_ref[:, at] * 4 + place_ref[:, at]))
         hot = hot_rows(down(relation_ref[:, at]))
         angle = dot(hot, parts[0]) + dot(hot, parts[1]) + dot(hot, parts[2])
         t = angle * angle
@@ -306,22 +306,31 @@
             spread.take_a(q, j)
         for k in (1, 3, 2):
             push(4 * k + j, (ga + 4 - k) % 4, (gb + j) % 4)
+    def squares(c, i):
+        t = table_ref[c, span(i, STEP)].astype(F32)
+        s = jnp.sum(t * t, axis=1, keepdims=True)
+        return jnp.transpose(jnp.broadcast_to(s, (STEP, STEP)))[0:8]
+
+    def half_first(i, _):
+        square_ref[i] = squares(core, i)
+        return 0
+
+    def half_second(i, _):
+        square_ref[i] = square_ref[i] + squares(other, i)
+        return 0
+
+    lax.fori_loop(0, 8, half_first, 0)
+    head_ref[core] = dot(hot_ref[...], table_ref[core])
     for i in range(16):
         w.wait(tp[i], table_ref.at[other, pl.ds(0, 64)], partner)
 
-    def squares(i, _):
-        re, im = table_ref[0, span(i, STEP)].astype(F32), table_ref[1, span(i, STEP)].astype(F32)
-        s = jnp.sum(re * re + im * im, axis=1, keepdims=True)
-        square_ref[i] = jnp.transpose(jnp.broadcast_to(s, (STEP, STEP)))[0:8]
-        return 0
-
-    lax.fori_loop(0, 8, squares, 0)
+    lax.fori_loop(0, 8, half_second, 0)
+    head_ref[other] = dot(hot_ref[...], table_ref[other])
 
     def main(i, _):
         at = span(i, MAIN)
-        hot = hot_rows(head_ref[at])
         c, s = cos_ref[at], sin_ref[at]
-        hr, hm = dot(hot, table_ref[0]), dot(hot, table_ref[1])
+        hr, hm = head_ref[0, at], head_ref[1, at]
         qr = hr * c - hm * s
         qm = hr * s + hm * c
         query_r, query_m = qr.astype(BF16), qm.astype(BF16)
@@ -534,7 +543,8 @@
             VMEM((TRIPLES, COLS), F32),
             VMEM((TRIPLES, COLS), F32),
             VMEM((TRIPLES, STEP), jnp.int32),
-            VMEM((TRIPLES, STEP), jnp.int32),
+            VMEM((TRIPLES, 1024), BF16),
+            VMEM((2, TRIPLES, COLS), F32),
             VMEM((2, 1024, COLS), BF16),
             VMEM((8, 8, STEP), F32),
             VMEM((2, TRIPLES, COLS), BF16),
@@ -561,7 +571,7 @@
             VMEM((4, 16, COLS), F32),
             VMEM((4, 4, 16, COLS), WIRE),
         ],
-        compiler_params=pltpu.CompilerParams(collective_id=0, has_side_effects=True, vmem_limit_bytes=36 << 20),
+        compiler_params=pltpu.CompilerParams(collective_id=0, has_side_effects=True, vmem_limit_bytes=42 << 20),
         name="step",
     )(*(pltpu.with_memory_space_constraint(v, pltpu.HBM) for v in (
         known_tails.T, head_owner.reshape(1, TRIPLES), head_row.reshape(1, TRIPLES), relation.reshape(1, TRIPLES),

time: 68.2 us -> 70.5 us (1.034)
  Pallas kernels: 65.2 us -> 67.6 us
    pallas_call x1, Pallas kernels: 65.2 us -> 67.6 us  [local(): pl.pallas_call(step_kernel, out_shape=(jax.ShapeDtypeStruct((4, 2 * COLS)...]
where the time goes in v6:
time: 70.5 us; the launch traced here: 70.4 us
  Pallas kernels  67.6 us (96%)
  other arithmetic  1.61 us (2%)
    pallas_call x1, Pallas kernels, local(): pl.pallas_call(step_kernel, out_shape=(jax.ShapeDtypeStruct((4, 2 * COLS)...  67.6 us
    convert_element_type x1, other arithmetic, local(): return (e, r.astype(F32))  1.61 us

profile of v6, /device:TPU:1, one launch (start us, length us, event | category | flops | bytes accessed | tf_op | source)
XLA Modules:
  0.0 70.4 jit_solution(103893821757961519)
XLA Ops:
  0.6 67.6 %step.1 = (f32[4,1024]{1,0:T(4,128)S(1)}, bf16[1024,512]{1,0:T(8,128)(2,1)S(1)}) custom-call(s32[32,512]{1,0:T(8,128)} %bitcast.5, s32[1,512]{1,0:T(1,128)} %bitcast.6, s32[1,512]{1,0:T(1,128)} %bitcast.7, s32[1,512]{1,0:T(1,128)} %bitcast.8, s32[1,512]{1,0:T(1,128)} %bitcast.9, f32[1024,512]{1,0:T(8,128)} %phases_hbm.1, bf16[16,1024]{1,0:T(8,128)(2,1)} %entity_hbm.1), custom_call_target="tpu_custom_call" | custom-call | tf_op jit(solution)/shard_map/step/pallas_call | solution.py:527
  68.2 1.6 %convert_element_type.3 = f32[1024,512]{1,0:T(8,128)} convert(bf16[1024,512]{1,0:T(8,128)(2,1)S(1)} %get-tuple-element.5) | non-fusion elementwise | flops 524288 | bytes 3145728 | tf_op jit(solution)/shard_map/convert_element_type | solution.py:579
  69.8 0.6 copy.10

commit v7 on v5

--- a/solution.py
+++ b/solution.py
@@ -273,7 +273,7 @@
 
     def prepare(i, _):
         at = span(i, STEP)
-        head_ref[at] = down(owner_ref[:, at] * 4 + place_ref[:, at])
+        head_ref[at] = hot_rows(down(owner_ref[:, at] * 4 + place_ref[:, at]))
         hot = hot_rows(down(relation_ref[:, at]))
         angle = dot(hot, parts[0]) + dot(hot, parts[1]) + dot(hot, parts[2])
         t = angle * angle
@@ -319,7 +319,7 @@
 
     def main(i, _):
         at = span(i, MAIN)
-        hot = hot_rows(head_ref[at])
+        hot = head_ref[at]
         c, s = cos_ref[at], sin_ref[at]
         hr, hm = dot(hot, table_ref[0]), dot(hot, table_ref[1])
         qr = hr * c - hm * s
@@ -534,7 +534,7 @@
             VMEM((TRIPLES, COLS), F32),
             VMEM((TRIPLES, COLS), F32),
             VMEM((TRIPLES, STEP), jnp.int32),
-            VMEM((TRIPLES, STEP), jnp.int32),
+            VMEM((TRIPLES, 1024), BF16),
             VMEM((2, 1024, COLS), BF16),
             VMEM((8, 8, STEP), F32),
             VMEM((2, TRIPLES, COLS), BF16),
@@ -561,7 +561,7 @@
             VMEM((4, 16, COLS), F32),
             VMEM((4, 4, 16, COLS), WIRE),
         ],
-        compiler_params=pltpu.CompilerParams(collective_id=0, has_side_effects=True, vmem_limit_bytes=36 << 20),
+        compiler_params=pltpu.CompilerParams(collective_id=0, has_side_effects=True, vmem_limit_bytes=40 << 20),
         name="step",
     )(*(pltpu.with_memory_space_constraint(v, pltpu.HBM) for v in (
         known_tails.T, head_owner.reshape(1, TRIPLES), head_row.reshape(1, TRIPLES), relation.reshape(1, TRIPLES),

time: 68.2 us -> 68.2 us (level)
  no operation moved by 1% of the time
where the time goes in v7:
time: 68.2 us; the launch traced here: 68.1 us
  Pallas kernels  65.3 us (96%)
  other arithmetic  1.61 us (2%)
    pallas_call x1, Pallas kernels, local(): pl.pallas_call(step_kernel, out_shape=(jax.ShapeDtypeStruct((4, 2 * COLS)...  65.3 us
    convert_element_type x1, other arithmetic, local(): return (e, r.astype(F32))  1.61 us

profile of v7, /device:TPU:1, one launch (start us, length us, event | category | flops | bytes accessed | tf_op | source)
XLA Modules:
  0.0 68.1 jit_solution(17395927052100231505)
XLA Ops:
  0.6 65.3 %step.1 = (f32[4,1024]{1,0:T(4,128)S(1)}, bf16[1024,512]{1,0:T(8,128)(2,1)S(1)}) custom-call(s32[32,512]{1,0:T(8,128)} %bitcast.5, s32[1,512]{1,0:T(1,128)} %bitcast.6, s32[1,512]{1,0:T(1,128)} %bitcast.7, s32[1,512]{1,0:T(1,128)} %bitcast.8, s32[1,512]{1,0:T(1,128)} %bitcast.9, f32[1024,512]{1,0:T(8,128)} %phases_hbm.1, bf16[16,1024]{1,0:T(8,128)(2,1)} %entity_hbm.1), custom_call_target="tpu_custom_call" | custom-call | tf_op jit(solution)/shard_map/step/pallas_call | solution.py:518
  65.9 1.6 %convert_element_type.3 = f32[1024,512]{1,0:T(8,128)} convert(bf16[1024,512]{1,0:T(8,128)(2,1)S(1)} %get-tuple-element.5) | non-fusion elementwise | flops 524288 | bytes 3145728 | tf_op jit(solution)/shard_map/convert_element_type | solution.py:569
  67.5 0.6 copy.10
